TPU v7x, 32 devices: a whole 2x2x4 slice. The times are simulated.
32 devices in a mesh: parts: 2 (over y), coef: 4 (over z), poly: 2 (over x), limb: 2 (over core).
Axes of the slice: x: 2, y: 2, z: 4, core: 2. Of those that a mesh axis runs over, the one named last changes fastest.
Arguments:
- coefficients: float32 [96, 128, 4096], P(('parts', 'poly', 'limb'), None, 'coef'), parts along dimension 0, may hold values from -6 to 6
- batch_weights: float32 [32, 48], P('parts', ('poly', 'limb')), parts along dimension 0, may hold values from -0.875 to 0.875
- claimed: float32 [2, 32, 48], P(None, 'parts', ('poly', 'limb')), parts along dimension 1, may hold values from -6 to 6
- point_index: int32 [32], P(('parts', 'poly', 'limb')), parts along dimension 0, may hold values from 0 to 524287
- point_cycle: int32 [32], P(('parts', 'poly', 'limb')), parts along dimension 0, may hold values from 0 to 3
Outputs:
- evaluations: float32 [2, 128, 96, 32, 128], P(None, 'coef', ('parts', 'poly', 'limb')), parts along dimension 2
- quotient: float32 [2, 32, 128, 4096], P(None, ('parts', 'poly', 'limb'), None, 'coef'), parts along dimension 1
There are 2 independent parts, one for each index of `parts`. A program takes and returns all parts, laid end to end along the dimension named above; each array names one. Nothing has to cross between parts.
All inputs are finite; a program needn't handle non-finite values.
Results may differ from a plain program's by a relative error of at most 0.0003.
Values sent between devices are 32-bit elements; how exact they have to be, the bound alone decides.
A program may use at most 128 MiB of HBM per device.

v0:
```python
import math

import jax
import jax.numpy as jnp
from jax import lax
from jax.sharding import PartitionSpec as P

LEN_COLS = 128
SPLIT_HI = 32
SPLIT_LO = 128
LEN_ROWS = 4096
LENGTH = 524288


precise = lax.Precision.HIGHEST


def phase_table(row_index, col_index, length):
    product = row_index[:, None] * col_index[None, :] % length
    angles = product.astype(jnp.float32) * (2.0 * math.pi / length)
    return (jnp.cos(angles), jnp.sin(angles))


def dft_table(length):
    indices = jnp.arange(length, dtype=jnp.int32)
    cos_table, sin_table = phase_table(indices, indices, length)
    factor = 1.0 / math.sqrt(length)
    return (cos_table * factor, sin_table * factor)


def row_turns():
    return phase_table(
        jnp.arange(SPLIT_HI, dtype=jnp.int32), jnp.arange(SPLIT_LO, dtype=jnp.int32), LEN_ROWS
    )


def contract(pattern, tables, pieces, inverse):
    cos_table, sin_table = tables
    real_part, imag_part = pieces

    def product(matrix, operand):
        return jnp.einsum(pattern, matrix, operand, precision=precise)

    if inverse:
        return (
            product(cos_table, real_part) - product(sin_table, imag_part),
            product(cos_table, imag_part) + product(sin_table, real_part),
        )
    return (
        product(cos_table, real_part) + product(sin_table, imag_part),
        product(cos_table, imag_part) - product(sin_table, real_part),
    )


def rotate(pieces, tables, inverse):
    cos_turn, sin_turn = tables
    real_part, imag_part = pieces
    if inverse:
        sin_turn = -sin_turn
    return (
        real_part * cos_turn + imag_part * sin_turn,
        imag_part * cos_turn - real_part * sin_turn,
    )


def first_section(values):
    extent = values.shape[1]
    rows_here = values.shape[2]
    cos_table, sin_table = dft_table(extent)
    real_part = jnp.einsum("kn,pnm->kpm", cos_table, values, precision=precise)
    imag_part = -jnp.einsum("kn,pnm->kpm", sin_table, values, precision=precise)
    row_index = lax.axis_index("coef") * rows_here + jnp.arange(rows_here, dtype=jnp.int32)
    frequency = jnp.arange(extent, dtype=jnp.int32)
    cos_turn, sin_turn = phase_table(frequency, row_index, LENGTH)
    pieces = rotate((real_part, imag_part), (cos_turn[:, None, :], sin_turn[:, None, :]), False)
    return jnp.stack(pieces)


def second_section(received):
    leading = received.shape[1:3]
    shaped = received.reshape((2,) + leading + (SPLIT_HI, SPLIT_LO))
    pieces = contract("va,kpab->kpvb", dft_table(SPLIT_HI), (shaped[0], shaped[1]), False)
    pieces = rotate(pieces, row_turns(), False)
    pieces = contract("ub,kpvb->kpvu", dft_table(SPLIT_LO), pieces, False)
    return jnp.stack(pieces)


def quotient_values(numerator, point_index, point_cycle):
    extent = numerator.shape[1]
    frequency = lax.axis_index("coef") * extent + jnp.arange(extent, dtype=jnp.int32)
    slow_part = jnp.arange(SPLIT_HI, dtype=jnp.int32)[None, :, None]
    fast_part = jnp.arange(SPLIT_LO, dtype=jnp.int32)[None, None, :]
    positions = LEN_COLS * (SPLIT_HI * fast_part + slow_part) + frequency[:, None, None]
    angles = positions.astype(jnp.float32) * (2.0 * math.pi / LENGTH)
    point_angle = point_index.astype(jnp.float32) * (2.0 * math.pi / LENGTH)
    radius = 1.0 + (point_cycle.astype(jnp.float32) + 1.0) / 512.0
    diff_real = jnp.cos(angles)[:, None] - (radius * jnp.cos(point_angle))[None, :, None, None]
    diff_imag = (radius * jnp.sin(point_angle))[None, :, None, None] - jnp.sin(angles)[:, None]
    magnitude = diff_real * diff_real + diff_imag * diff_imag
    quot_real = (numerator[0] * diff_real + numerator[1] * diff_imag) / magnitude
    quot_imag = (numerator[1] * diff_real - numerator[0] * diff_imag) / magnitude
    return (quot_real, quot_imag)


def inverse_front(pieces):
    extent = pieces[0].shape[0]
    pieces = contract("ub,kjvu->kjvb", dft_table(SPLIT_LO), pieces, True)
    pieces = rotate(pieces, row_turns(), True)
    pieces = contract("va,kjvb->kjab", dft_table(SPLIT_HI), pieces, True)
    leading = pieces[0].shape[:2]
    pieces = (pieces[0].reshape(leading + (LEN_ROWS,)), pieces[1].reshape(leading + (LEN_ROWS,)))
    frequency = lax.axis_index("coef") * extent + jnp.arange(extent, dtype=jnp.int32)
    cos_turn, sin_turn = phase_table(frequency, jnp.arange(LEN_ROWS, dtype=jnp.int32), LENGTH)
    pieces = rotate(pieces, (cos_turn[:, None, :], sin_turn[:, None, :]), True)
    return jnp.stack(pieces)


def inverse_first(received):
    pieces = contract("kn,kjm->jnm", dft_table(LEN_COLS), (received[0], received[1]), True)
    return jnp.stack(pieces)


def shards(coefficients, batch_weights, claimed, point_index, point_cycle):
    sectioned = first_section(coefficients)
    evaluations = second_section(
        lax.all_to_all(sectioned, "coef", split_axis=1, concat_axis=3, tiled=True)
    )
    offsets = jnp.sum(batch_weights[None] * claimed, axis=2)
    combined = jnp.einsum("jp,pnm->jnm", batch_weights, coefficients, precision=precise)
    combined_here, offsets_here = (
        lax.psum_scatter(combined, ("poly", "limb"), scatter_dimension=0, tiled=True),
        lax.psum_scatter(offsets, ("poly", "limb"), scatter_dimension=1, tiled=True),
    )
    column_sectioned = first_section(combined_here)
    numerator = second_section(
        lax.all_to_all(column_sectioned, "coef", split_axis=1, concat_axis=3, tiled=True)
    )
    numerator = numerator - offsets_here[:, None, :, None, None]
    quot_pieces = quotient_values(numerator, point_index, point_cycle)
    returned = inverse_front(quot_pieces)
    quotient = inverse_first(
        lax.all_to_all(returned, "coef", split_axis=3, concat_axis=1, tiled=True)
    )
    return (evaluations, quotient)


def solution(mesh):
    placed = (
        P(("parts", "poly", "limb"), None, "coef"),
        P("parts", ("poly", "limb")),
        P(None, "parts", ("poly", "limb")),
        P(("parts", "poly", "limb")),
        P(("parts", "poly", "limb")),
    )
    return jax.shard_map(
        shards,
        mesh=mesh,
        in_specs=placed,
        out_specs=(
            P(None, "coef", ("parts", "poly", "limb"), None, None),
            P(None, ("parts", "poly", "limb"), None, "coef"),
        ),
        check_vma=False,
    )
```

profile of v0, /device:TPU:0, one launch (start us, length us, event | category | flops | bytes accessed | tf_op | source)
XLA Modules:
  0.0 710.6 jit_solution(118447262701700206)
XLA Ops:
  7.2 15.2 %fusion = f32[16,128,1024]{2,0,1:T(8,128)S(1)} fusion(f32[12,128,1024]{2,1,0:T(8,128)} %param.5, f32[16,12]{1,0:T(8,128)} %param.6), kind=kOutput, calls=%fused_computation.3 | convolution fusion | flops 301989888 | bytes 14680832 | tf_op jit(solution)/shard_map/jp,pnm->jnm/dot_general | solution.py:129
  22.4 8.3 %copy.107 = f32[16,128,1024]{2,1,0:T(8,128)} copy(f32[16,128,1024]{2,0,1:T(8,128)S(1)} %fusion) | data formatting | bytes 16777216 | tf_op jit(solution)/shard_map/jp,pnm->jnm/dot_general | solution.py:129
  30.7 2.0 fusion.35
  32.8 72.2 %reduce-scatter.3.cloned.1.call-done = f32[4,128,1024]{2,1,0:T(8,128)} async-done(((f32[16,128,1024]{2,1,0:T(8,128)}), f32[4,128,1024]{2,1,0:T(8,128)}) %reduce-scatter.3.cloned.1.call-update) | async-done | bytes 2097168 | tf_op jit(solution)/shard_map/reduce_scatter | solution.py:131
  105.0 3.8 fusion.57
  108.8 2.6 add_bitcast_fusion.5
  112.2 4.7 copy.108
  116.9 5.0 all-to-all-start.1
  121.9 8.6 %fusion.59 = f32[128,12,1024]{2,0,1:T(8,128)S(1)} fusion(f32[12,128,1024]{2,1,0:T(8,128)} %param.5), kind=kOutput, calls=%fused_computation.110 | convolution fusion | flops 2416164864 | bytes 12582912 | tf_op jit(solution)/shard_map/kn,pnm->kpm/dot_general | solution.py:71
  130.6 10.1 %add_bitcast_fusion.1 = (f32[1,128,12,1024]{3,1,2,0:T(8,128)}, f32[1,128,12,1024]{3,1,2,0:T(8,128)}) fusion(f32[128,12,1024]{2,0,1:T(8,128)S(1)} %fusion.59, f32[128,1024]{1,0:T(8,128)S(1)} %get-tuple-element.31, f32[128,1024]{1,0:T(8,128)S(1)} %get-tuple-element.30, f32[12,128,1024]{2,1,0:T(8,128)S(1)} %bitcast.217), kind=kOutput, calls=%fused_computation.14 | convolution fusion | flops 2427174912 | bytes 26214400 | tf_op jit(solution)/shard_map/kn,pnm->kpm/dot_general | solution.py:70
  140.7 12.1 %pad_maximum_fusion = f32[2,128,12,1024]{3,1,2,0:T(8,128)} fusion(f32[1,128,12,1024]{3,1,2,0:T(8,128)} %get-tuple-element.15, f32[1,128,12,1024]{3,1,2,0:T(8,128)} %get-tuple-element.14), kind=kLoop, calls=%fused_computation | loop fusion | flops 3145728 | bytes 25165824 | tf_op jit(solution)/shard_map/stack | solution.py:76
  152.9 22.0 %copy.100 = f32[2,128,12,1024]{3,0,2,1:T(2,128)} copy(f32[2,128,12,1024]{3,1,2,0:T(8,128)} %pad_maximum_fusion) | data formatting | bytes 25165824 | tf_op jit(solution)/shard_map/stack | solution.py:76
  174.9 40.3 %all-to-all-done.1 = f32[2,128,4,1024]{3,2,0,1:T(4,128)} async-done(((f32[2,128,4,1024]{3,2,0,1:T(4,128)}), f32[2,128,4,1024]{3,2,0,1:T(4,128)}, u32[]{:S(2)}, u32[]{:S(2)}) %all-to-all-start.1) | async-done | bytes 4194336 | tf_op jit(solution)/shard_map/all_to_all | solution.py:136
  215.2 6.3 all-to-all-start
  222.9 6.2 all-reduce
  229.5 3.1 fusion.28
  232.6 2.1 fusion.33
  234.7 6.1 copy.163
  240.8 3.0 fusion.268
  243.8 2.1 squeeze.29
  245.9 3.2 squeeze.28
  257.3 2.2 fusion.13
  259.5 2.6 subtract_bitcast_fusion.4
  262.1 2.2 fusion.17
  264.2 2.2 add_bitcast_fusion.4
  269.0 2.1 fusion.47
  271.1 2.1 fusion.45
  273.2 2.3 convolution_subtract_fusion.1
  275.5 2.1 convolution_add_fusion.1
  277.6 2.2 fusion.12
  279.8 3.6 add_bitcast_fusion.3
  283.4 3.1 reshape.267
  286.5 3.9 fusion.11
  290.5 3.6 subtract_bitcast_fusion.3
  294.1 3.1 reshape.266
  297.2 3.9 multiply_add_fusion
  301.1 2.3 pad_maximum_fusion.3
  303.4 13.5 %copy.119 = f32[2,32,4,4096]{1,2,0,3:T(4,128)} copy(f32[2,32,4,4096]{3,1,2,0:T(8,128)} %pad_maximum_fusion.3) | data formatting | bytes 8388608 | tf_op jit(solution)/shard_map/stack | solution.py:115
  316.9 14.5 %reshape.286 = f32[4,1,262144]{2,1,0:T(1,128)} reshape(f32[4096,2,4,32]{3,2,1,0:T(4,128)} %bitcast.218) | data formatting | bytes 8388608
  331.4 162.7 %all-to-all-done = f32[2,128,12,1024]{3,0,2,1:T(2,128)} async-done(((f32[2,128,12,1024]{3,0,2,1:T(2,128)}), f32[2,128,12,1024]{3,0,2,1:T(2,128)}, u32[]{:S(2)}, u32[]{:S(2)}) %all-to-all-start) | async-done | bytes 12582944 | tf_op jit(solution)/shard_map/all_to_all | solution.py:126
  494.1 5.3 all-to-all-start.2
  499.3 16.4 %copy.162 = f32[2,4,32,12,1024]{4,1,3,2,0:T(4,128)} copy(f32[2,4,32,12,1024]{4,0,3,2,1:T(2,128)} %bitcast.4) | data formatting | bytes 25165824 | tf_op jit(solution)/shard_map/all_to_all | solution.py:126
  515.8 14.8 %fusion.266 = (f32[1,32,12,4,1024]{4,3,2,1,0:T(4,128)}, f32[1,32,12,4,1024]{4,3,2,1,0:T(4,128)}) fusion(f32[2,32,12,4,1024]{4,3,2,1,0:T(4,128)} %bitcast.224), kind=kLoop, calls=%fused_computation.337 | loop fusion | bytes 25165824 | tf_op jit(solution)/shard_map/slice | solution.py:82
  530.6 7.9 %squeeze.26 = f32[32,12,32,128]{3,2,1,0:T(8,128)} reshape(f32[1,32,12,4,1024]{4,3,2,1,0:T(4,128)} %get-tuple-element.16) | data formatting | bytes 12582912 | tf_op jit(solution)/shard_map/squeeze | solution.py:82
  538.5 8.0 %squeeze.27 = f32[32,12,32,128]{3,2,1,0:T(8,128)} reshape(f32[1,32,12,4,1024]{4,3,2,1,0:T(4,128)} %get-tuple-element.17) | data formatting | bytes 12582912 | tf_op jit(solution)/shard_map/squeeze | solution.py:82
  546.5 9.9 %fusion.82 = f32[32,12,128,32]{2,3,1,0:T(8,128)} fusion(f32[32,12,32,128]{3,2,1,0:T(8,128)} %squeeze.26), kind=kOutput, calls=%fused_computation.141 | convolution fusion | flops 603995136 | bytes 12582912 | tf_op jit(solution)/shard_map/va,kpab->kpvb/dot_general | solution.py:42
  556.4 7.6 %fusion.94 = f32[32,12,128,32]{2,3,1,0:T(8,128)} fusion(f32[32,12,32,128]{3,2,1,0:T(8,128)S(1)} %bitcast.221), kind=kOutput, calls=%fused_computation.153 | convolution fusion | flops 603995136 | bytes 12582912 | tf_op jit(solution)/shard_map/va,kpab->kpvb/dot_general | solution.py:42
  564.0 7.5 %fusion.84 = f32[32,12,128,32]{2,3,1,0:T(8,128)} fusion(f32[32,12,32,128]{3,2,1,0:T(8,128)S(1)} %bitcast.223), kind=kOutput, calls=%fused_computation.143 | convolution fusion | flops 603995136 | bytes 12582912 | tf_op jit(solution)/shard_map/va,kpab->kpvb/dot_general | solution.py:42
  571.5 12.9 %fusion.2 = (f32[32,12,32,128]{3,2,1,0:T(8,128)}, f32[32,12,32,128]{3,2,1,0:T(8,128)S(1)}) fusion(f32[32,128]{1,0:T(8,128)S(1)} %get-tuple-element.36, f32[32,128]{1,0:T(8,128)S(1)} %get-tuple-element.37, f32[32,12,128,32]{2,3,1,0:T(8,128)} %fusion.82, f32[32,12,128,32]{2,3,1,0:T(8,128)} %fusion.94, f32[32,12,128,32]{2,3,1,0:T(8,128)} %fusion.84, ...), kind=kOutput, calls=%fused_computation.7 | convolution fusion | flops 616578048 | bytes 37781504 | tf_op jit(solution)/shard_map/va,kpab->kpvb/dot_general | solution.py:42
  584.4 5.7 fusion.51
  590.1 5.7 fusion.53
  595.8 8.0 %subtract_bitcast_fusion = f32[1,32,12,32,128]{4,3,2,1,0:T(8,128)} fusion(f32[32,12,32,128]{3,2,1,0:T(8,128)S(1)} %fusion.51, f32[32,12,32,128]{3,2,1,0:T(8,128)S(1)} %copy-done), kind=kOutput, calls=%fused_computation.11 | convolution fusion | flops 2417737728 | bytes 18874368 | tf_op jit(solution)/shard_map/ub,kpvb->kpvu/dot_general | solution.py:42
  603.9 7.6 %add_bitcast_fusion = f32[1,32,12,32,128]{4,3,2,1,0:T(8,128)} fusion(f32[32,12,32,128]{3,2,1,0:T(8,128)S(1)} %fusion.53, f32[32,12,32,128]{3,2,1,0:T(8,128)S(1)} %get-tuple-element.13), kind=kOutput, calls=%fused_computation.12 | convolution fusion | flops 2417737728 | bytes 18874368 | tf_op jit(solution)/shard_map/ub,kpvb->kpvu/dot_general | solution.py:42
  611.4 12.2 %pad_maximum_fusion.1 = f32[2,32,12,32,128]{4,3,2,1,0:T(8,128)} fusion(f32[1,32,12,32,128]{4,3,2,1,0:T(8,128)} %subtract_bitcast_fusion, f32[1,32,12,32,128]{4,3,2,1,0:T(8,128)} %add_bitcast_fusion), kind=kLoop, calls=%fused_computation.1 | loop fusion | flops 3145728 | bytes 25165824 | tf_op jit(solution)/shard_map/stack | solution.py:85
  624.1 15.4 %reduce = f32[4,262144]{1,0:T(4,128)} reduce(f32[4,1,262144]{2,1,0:T(1,128)} %all-to-all-done.2, f32[]{:T(128)} %broadcast.735), dimensions={1}, to_apply=%all_to_all.39.reduce_sub_computation | reduce | bytes 8388612 | tf_op jit(solution)/shard_map/all_to_all | solution.py:142
  639.5 20.9 %reshape.287 = f32[4096,2,4,32]{3,2,1,0:T(4,128)} reshape(f32[4,262144]{1,0:T(4,128)} %reduce) | data formatting | bytes 8388608
  660.3 15.1 %copy.152 = f32[2,32,4,4,1024]{4,3,1,2,0:T(4,128)} copy(f32[2,32,4,4,1024]{1,2,0,4,3:T(4,128)} %bitcast.219) | data formatting | bytes 8388608 | tf_op jit(solution)/shard_map/all_to_all | solution.py:142
  675.4 3.2 fusion.267
  679.8 3.6 fusion.61
  684.7 3.6 fusion.63
  688.2 3.8 add_bitcast_fusion.2
  692.1 3.6 subtract_bitcast_fusion.2
  695.7 2.2 pad_maximum_fusion.4
  697.9 5.3 copy.127
  (65 shorter events, 15.4 us)
Async XLA Ops:
  7.2 97.8 %reduce-scatter.3.cloned.1.call-start = ((), (), s32[]{:S(2)}) async-start(), calls=%async_computation.4 | async-start | bytes 10485760 | tf_op jit(solution)/shard_map/reduce_scatter | solution.py:131
  105.0 3.9 copy-start.4
  116.9 13.7 %slice-start = ((s8[6291456]{0:T(1024)(128)(4,1)}), s8[2097152]{0:T(1024)(128)(4,1)S(1)}, s32[]{:S(2)}) async-start(s8[6291456]{0:T(1024)(128)(4,1)} %bitcast.216), calls=%async_computation.5 | async-start | bytes 4194304
  116.9 98.3 %all-to-all-start.1 = ((f32[2,128,4,1024]{3,2,0,1:T(4,128)}), f32[2,128,4,1024]{3,2,0,1:T(4,128)}, u32[]{:S(2)}, u32[]{:S(2)}) async-start(f32[2,128,4,1024]{3,2,0,1:T(4,128)} %copy.108), calls=%async_computation.2 | async-start | bytes 8388608 | tf_op jit(solution)/shard_map/all_to_all | solution.py:136
  121.9 8.7 %slice-start.1 = ((s8[6291456]{0:T(1024)(128)(4,1)}), s8[4194304]{0:T(1024)(128)(4,1)S(1)}, s32[]{:S(2)}) async-start(s8[6291456]{0:T(1024)(128)(4,1)} %bitcast.216), calls=%async_computation.6 | async-start | bytes 8388608
  174.9 46.6 %copy-start.8 = (f32[16,12]{1,0:T(8,128)S(1)}, f32[16,12]{1,0:T(8,128)}, u32[]{:S(2)}) copy-start(f32[16,12]{1,0:T(8,128)} %param.6) | copy-start | bytes 2308
  174.9 46.7 %copy-start.12 = (u32[32]{0:T(128)S(1)}, u32[32]{0:T(128)}, u32[]{:S(2)}) copy-start(u32[32]{0:T(128)} %constant.131) | copy-start | bytes 388
  174.9 48.0 %copy-start.9 = (f32[2,16,12]{1,0,2:T(2,128)S(1)}, f32[2,16,12]{1,0,2:T(2,128)}, u32[]{:S(2)}) copy-start(f32[2,16,12]{1,0,2:T(2,128)} %param.7) | copy-start | bytes 4612
  174.9 54.5 %copy-start.10 = (s32[4]{0:T(128)S(1)}, s32[4]{0:T(128)}, u32[]{:S(2)}) copy-start(s32[4]{0:T(128)} %param.8) | copy-start | bytes 52
  174.9 54.5 %copy-start.11 = (s32[4]{0:T(128)S(1)}, s32[4]{0:T(128)}, u32[]{:S(2)}) copy-start(s32[4]{0:T(128)} %param.9) | copy-start | bytes 52
  215.2 278.8 %all-to-all-start = ((f32[2,128,12,1024]{3,0,2,1:T(2,128)}), f32[2,128,12,1024]{3,0,2,1:T(2,128)}, u32[]{:S(2)}, u32[]{:S(2)}) async-start(f32[2,128,12,1024]{3,0,2,1:T(2,128)} %copy.100), calls=%async_computation | async-start | bytes 25165824 | tf_op jit(solution)/shard_map/all_to_all | solution.py:126
  249.1 2.0 copy-start.3
  266.4 1.0 copy-start.6
  266.5 1.2 copy-start.7
  277.6 2.2 copy-start.1
  286.5 3.9 copy-start.2
  294.1 3.1 copy-start.5
  494.1 129.5 %all-to-all-start.2 = ((f32[4,1,262144]{2,1,0:T(1,128)}), f32[4,1,262144]{2,1,0:T(1,128)}, u32[]{:S(2)}, u32[]{:S(2)}) async-start(f32[4,1,262144]{2,1,0:T(1,128)} %reshape.286), calls=%async_computation.3 | async-start | bytes 8388608 | tf_op jit(solution)/shard_map/all_to_all | solution.py:142
  538.5 17.9 %slice-start.2 = ((s8[6291456]{0:T(1024)(128)(4,1)}), s8[2097152]{0:T(1024)(128)(4,1)S(1)}, s32[]{:S(2)}) async-start(s8[6291456]{0:T(1024)(128)(4,1)} %bitcast.220), calls=%async_computation.7 | async-start | bytes 4194304
  546.5 9.9 %slice-start.3 = ((s8[6291456]{0:T(1024)(128)(4,1)}), s8[4194304]{0:T(1024)(128)(4,1)S(1)}, s32[]{:S(2)}) async-start(s8[6291456]{0:T(1024)(128)(4,1)} %bitcast.220), calls=%async_computation.8 | async-start | bytes 8388608
  546.5 17.5 %slice-start.4 = ((s8[6291456]{0:T(1024)(128)(4,1)}), s8[4194304]{0:T(1024)(128)(4,1)S(1)}, s32[]{:S(2)}) async-start(s8[6291456]{0:T(1024)(128)(4,1)} %bitcast.222), calls=%async_computation.9 | async-start | bytes 8388608
  556.4 7.6 %slice-start.5 = ((s8[6291456]{0:T(1024)(128)(4,1)}), s8[2097152]{0:T(1024)(128)(4,1)S(1)}, s32[]{:S(2)}) async-start(s8[6291456]{0:T(1024)(128)(4,1)} %bitcast.222), calls=%async_computation.10 | async-start | bytes 4194304
  584.4 5.7 copy-start
Sparse Core Ops, SparseCore 0:
  30.8 74.1 reduce-scatter.2
where the time goes:
time: 717 us; the launch traced here: 711 us
  waiting for transfers between devices  275 us (38%)
  local copies, waits for them, and re-layouts  180 us (25%)
  matrix products  159 us (22%)
  other arithmetic  58.2 us (8%)
  starting transfers between devices  16.6 us (2%)
  between operations  15.6 us (2%)
    all_to_all x1, waiting for transfers between devices, shards(): lax.all_to_all(sectioned, 'coef', split_axis=1, concat_axis=3, tiled=True)  163 us
    dot_general x28, matrix products, product(): return jnp.einsum(pattern, matrix, operand, precision=precise)  119 us
    reduce_scatter x1, waiting for transfers between devices, shards(): lax.psum_scatter(combined, ('poly', 'limb'), scatter_dimension=0, tiled=T...  72.2 us
    unnamed x44, local copies, waits for them, and re-layouts  42.1 us
    all_to_all x1, waiting for transfers between devices, shards(): lax.all_to_all(column_sectioned, 'coef', split_axis=1, concat_axis=3, til...  40.3 us
    another operation x2, local copies, waits for them, and re-layouts, first_section(): return jnp.stack(pieces)  26.8 us
    slice x2, local copies, waits for them, and re-layouts, second_section(): shaped[0]  17.8 us
    all_to_all x1, local copies, waits for them, and re-layouts, shards(): lax.all_to_all(sectioned, 'coef', split_axis=1, concat_axis=3, tiled=True)  16.4 us
  transfers between devices with their start and end apart: 4, of which 3 were waited for; matrix products, arithmetic and copies ran while one was open for 40% of the time, Pallas kernels for 0%

commit v1 on v0

v1 whole, which is shorter than its diff:
```python
import functools
import math

import jax
import jax.numpy as jnp
from jax import lax
from jax.experimental import pallas as pl
from jax.experimental.pallas import tpu as pltpu
from jax.sharding import PartitionSpec as P

SPLIT_HI = 32
SPLIT_LO = 128
CHUNKS = 4

precise = lax.Precision.HIGHEST


def phase_table(row_index, col_index, length):
    product = row_index[:, None] * col_index[None, :] % length
    angles = product.astype(jnp.float32) * (2.0 * math.pi / length)
    return (jnp.cos(angles), jnp.sin(angles))


def cost(flops, moved):
    return pl.CostEstimate(flops=flops, bytes_accessed=moved, transcendentals=0)


def first_kernel(mat_ref, cos_ref, sin_ref, x_ref, out_ref):
    targets, _, _, groups, per_target, lanes = out_ref.shape
    extent = targets * per_target
    for g in range(groups):
        cols = slice(g * lanes, (g + 1) * lanes)
        both = jnp.dot(mat_ref[...], x_ref[0, :, cols], precision=precise,
                       preferred_element_type=jnp.float32)
        real, imag = both[:extent], both[extent:]
        cos_turn, sin_turn = cos_ref[:, cols], sin_ref[:, cols]
        turned_real = real * cos_turn + imag * sin_turn
        turned_imag = imag * cos_turn - real * sin_turn
        for t in range(targets):
            rows = slice(t * per_target, (t + 1) * per_target)
            out_ref[t, 0, 0, g] = turned_real[rows]
            out_ref[t, 0, 1, g] = turned_imag[rows]


def first_section(values, tables, start, count, targets):
    matrix, cos_turn, sin_turn = tables
    _, extent, rows_here = values.shape
    groups = rows_here // SPLIT_LO
    per_target = extent // targets
    shape = (targets, count, 2, groups, per_target, SPLIT_LO)
    block = (targets, 1, 2, groups, per_target, SPLIT_LO)
    size = count * 2 * extent * rows_here
    return pl.pallas_call(
        first_kernel,
        grid=(count,),
        in_specs=[
            pl.BlockSpec((2 * extent, extent), lambda p: (0, 0)),
            pl.BlockSpec((extent, rows_here), lambda p: (0, 0)),
            pl.BlockSpec((extent, rows_here), lambda p: (0, 0)),
            pl.BlockSpec((1, extent, rows_here), lambda p: (start + p, 0, 0)),
        ],
        out_specs=pl.BlockSpec(block, lambda p: (0, p, 0, 0, 0, 0)),
        out_shape=jax.ShapeDtypeStruct(shape, jnp.float32),
        compiler_params=pltpu.CompilerParams(vmem_limit_bytes=24 << 20),
        cost_estimate=cost(size * extent * 12, size * 6),
        name="first_section",
    )(matrix, cos_turn, sin_turn, values)


def fft(pieces):
    count = len(pieces)
    if count == 1:
        return pieces
    even, odd = fft(pieces[0::2]), fft(pieces[1::2])
    low, high = [], []
    for k in range(count // 2):
        er, ei = even[k]
        orr, oi = odd[k]
        if k == 0:
            tr, ti = orr, oi
        elif 4 * k == count:
            tr, ti = oi, -orr
        else:
            c = math.cos(2 * math.pi * k / count)
            s = math.sin(2 * math.pi * k / count)
            if 8 * k == count:
                tr, ti = (orr + oi) * c, (oi - orr) * c
            elif 8 * k == 3 * count:
                tr, ti = (oi - orr) * s, (orr + oi) * (-s)
            else:
                tr, ti = orr * c + oi * s, oi * c - orr * s
        low.append((er + tr, ei + ti))
        high.append((er - tr, ei - ti))
    return low + high


def second_kernel(mat_ref, cos_ref, sin_ref, in_ref, *rest):
    out_ref, real_ref, imag_ref = rest[-3:]
    sources, _, _, groups, here, lanes = in_ref.shape
    pieces = [
        (in_ref[s, 0, 0, g], in_ref[s, 0, 1, g]) for s in range(sources) for g in range(groups)
    ]
    for v, (real, imag) in enumerate(fft(pieces)):
        cos_turn, sin_turn = cos_ref[v : v + 1], sin_ref[v : v + 1]
        at = pl.ds(v, here, stride=SPLIT_HI)
        real_ref[at, :] = real * cos_turn + imag * sin_turn
        imag_ref[at, :] = imag * cos_turn - real * sin_turn
    both = jnp.concatenate([real_ref[...], imag_ref[...]], axis=1)
    done = jnp.dot(both, mat_ref[...], precision=precise, preferred_element_type=jnp.float32)
    out_ref[0, :, 0] = done[:, :lanes].reshape(here, SPLIT_HI, lanes)
    out_ref[1, :, 0] = done[:, lanes:].reshape(here, SPLIT_HI, lanes)


def second_section(received, tables, start, total, held):
    matrix, cos_turn, sin_turn = tables
    sources, count, _, groups, per_target, lanes = received.shape
    here = min(8, per_target)
    out_shape = jax.ShapeDtypeStruct((2, per_target, total, SPLIT_HI, lanes), jnp.float32)
    size = received.size
    operands = [matrix, cos_turn, sin_turn, received]
    in_specs = [
        pl.BlockSpec(matrix.shape, lambda p, k: (0, 0)),
        pl.BlockSpec(cos_turn.shape, lambda p, k: (0, 0)),
        pl.BlockSpec(sin_turn.shape, lambda p, k: (0, 0)),
        pl.BlockSpec((sources, 1, 2, groups, here, lanes), lambda p, k: (0, p, 0, 0, k, 0)),
    ]
    aliases = {}
    if held is not None:
        operands.append(held)
        in_specs.append(pl.BlockSpec(memory_space=pl.ANY))
        aliases = {4: 0}
    return pl.pallas_call(
        second_kernel,
        grid=(count, per_target // here),
        in_specs=in_specs,
        out_specs=pl.BlockSpec(
            (2, here, 1, SPLIT_HI, lanes), lambda p, k: (0, k, start + p, 0, 0)
        ),
        out_shape=out_shape,
        scratch_shapes=[pltpu.VMEM((SPLIT_HI * here, lanes), jnp.float32)] * 2,
        input_output_aliases=aliases,
        compiler_params=pltpu.CompilerParams(vmem_limit_bytes=16 << 20),
        cost_estimate=cost(size * 2 * lanes * 12, size * 8),
        name="second_section",
    )(*operands)


def combine_kernel(weight_ref, x_ref, out_ref):
    columns, polys = weight_ref.shape
    for g in range(x_ref.shape[2] // SPLIT_LO):
        cols = slice(g * SPLIT_LO, (g + 1) * SPLIT_LO)
        rows = [x_ref[p, :, cols] for p in range(polys)]
        for j in range(columns):
            total = rows[0] * weight_ref[j, 0]
            for p in range(1, polys):
                total = total + rows[p] * weight_ref[j, p]
            out_ref[j, :, cols] = total


def combine(weights, values):
    polys, extent, rows_here = values.shape
    columns = weights.shape[0]
    size = extent * rows_here
    return pl.pallas_call(
        combine_kernel,
        grid=(extent // 8,),
        in_specs=[
            pl.BlockSpec(memory_space=pltpu.SMEM),
            pl.BlockSpec((polys, 8, rows_here), lambda n: (0, n, 0)),
        ],
        out_specs=pl.BlockSpec((columns, 8, rows_here), lambda n: (0, n, 0)),
        out_shape=jax.ShapeDtypeStruct((columns, extent, rows_here), jnp.float32),
        compiler_params=pltpu.CompilerParams(vmem_limit_bytes=16 << 20),
        cost_estimate=cost(size * columns * polys * 20, size * 4 * (columns + polys)),
        name="combine",
    )(weights, values)


def powers(exponents, point_index, log_radius, length):
    shape = (-1,) + (1,) * exponents.ndim
    phase = (exponents[None] * point_index.reshape(shape)) & (length - 1)
    angles = phase.astype(jnp.float32) * (2.0 * math.pi / length)
    size = jnp.exp(-exponents[None].astype(jnp.float32) * log_radius.reshape(shape))
    return size * jnp.cos(angles), size * jnp.sin(angles)


def quotient_kernel(matrix_ref, step_ref, carry_ref, c_ref, out_ref):
    rows, width = c_ref.shape[1:]
    lanes = step_ref.shape[2]
    step_real, step_imag = step_ref[0, 0:1], step_ref[0, 1:2]
    carry = carry_ref[0]
    carry_real, carry_imag = carry[:, 0:1], carry[:, 1:2]
    for g in range(width // lanes):
        cols = slice(g * lanes, (g + 1) * lanes)
        local = jnp.dot(c_ref[0, :, cols], matrix_ref[0], precision=precise,
                        preferred_element_type=jnp.float32)
        real = local[:, :lanes] + (step_real * carry_real - step_imag * carry_imag)
        imag = local[:, lanes:] + (step_real * carry_imag + step_imag * carry_real)
        out_ref[0, 0, :, cols] = real
        out_ref[1, 0, :, cols] = imag
        carry_real, carry_imag = real[:, lanes - 1 :], imag[:, lanes - 1 :]


def quotient_section(combined, offsets, point_index, point_cycle, owners):
    columns, extent, rows_here = combined.shape
    length = extent * rows_here * owners
    lanes = SPLIT_LO
    log_radius = jnp.log1p((point_cycle.astype(jnp.float32) + 1.0) / 512.0)
    power = functools.partial(
        powers, point_index=point_index, log_radius=log_radius, length=length
    )
    index = jnp.arange(lanes, dtype=jnp.int32)
    ahead = index[None, :] - index[:, None] + 1
    below = (ahead > 0)[None]
    local_real, local_imag = power(jnp.maximum(ahead, 0))
    matrix = jnp.concatenate(
        [jnp.where(below, -local_real, 0.0), jnp.where(below, -local_imag, 0.0)], axis=2
    )
    step = jnp.stack(power(index + 1), axis=1)
    end_real, end_imag = power(rows_here - jnp.arange(rows_here, dtype=jnp.int32))
    ends = jnp.stack(
        [
            -jnp.sum(combined * end_real[:, None, :], axis=2),
            -jnp.sum(combined * end_imag[:, None, :], axis=2),
        ]
    )
    gathered = lax.all_gather(ends, "coef")
    me = lax.axis_index("coef")
    shift = offsets * math.sqrt(length)
    turn_real, turn_imag = power(jnp.full((), rows_here, jnp.int32))
    first = jnp.stack(
        [
            turn_real * shift[0] - turn_imag * shift[1],
            turn_real * shift[1] + turn_imag * shift[0],
        ]
    )
    gathered = gathered.at[0, :, :, 0].add(first)
    row = jnp.arange(extent, dtype=jnp.int32)
    owner = jnp.arange(owners, dtype=jnp.int32)
    segments = extent * owners
    away = (
        (row[:, None, None] * owners + me)
        - (row[None, None, :] * owners + owner[None, :, None])
        - 1
        + segments
    ) % segments
    pass_real, pass_imag = power(away * rows_here)
    whole = 1.0 - power(jnp.full((), length, jnp.int32))[0]
    ends_real = jnp.transpose(gathered[:, 0], (1, 0, 2))[:, None]
    ends_imag = jnp.transpose(gathered[:, 1], (1, 0, 2))[:, None]
    carry_real = jnp.sum(pass_real * ends_real - pass_imag * ends_imag, axis=(2, 3))
    carry_imag = jnp.sum(pass_real * ends_imag + pass_imag * ends_real, axis=(2, 3))
    carry = jnp.stack([carry_real, carry_imag], axis=2) / whole[:, None, None]
    starts = ((row == 0) & (me == 0))[None, :, None]
    carry = carry + jnp.where(starts, shift.T[:, None, :], 0.0)
    size = columns * extent * rows_here
    return pl.pallas_call(
        quotient_kernel,
        grid=(columns,),
        in_specs=[
            pl.BlockSpec((1, lanes, 2 * lanes), lambda j: (j, 0, 0)),
            pl.BlockSpec((1, 2, lanes), lambda j: (j, 0, 0)),
            pl.BlockSpec((1, extent, 2), lambda j: (j, 0, 0)),
            pl.BlockSpec((1, extent, rows_here), lambda j: (j, 0, 0)),
        ],
        out_specs=pl.BlockSpec((2, 1, extent, rows_here), lambda j: (0, j, 0, 0)),
        out_shape=jax.ShapeDtypeStruct((2, columns, extent, rows_here), jnp.float32),
        compiler_params=pltpu.CompilerParams(vmem_limit_bytes=16 << 20),
        cost_estimate=cost(size * 4 * lanes * 6, size * 12),
        name="quotient",
    )(matrix, step, carry, combined)


def transform_tables(extent, rows_here, length):
    index = jnp.arange(extent, dtype=jnp.int32)
    cos_table, sin_table = phase_table(index, index, extent)
    first_matrix = jnp.concatenate([cos_table, -sin_table]) * (1.0 / math.sqrt(extent))
    row_index = lax.axis_index("coef") * rows_here + jnp.arange(rows_here, dtype=jnp.int32)
    cos_turn, sin_turn = phase_table(index, row_index, length)
    slow = jnp.arange(SPLIT_HI, dtype=jnp.int32)
    fast = jnp.arange(SPLIT_LO, dtype=jnp.int32)
    cos_row, sin_row = phase_table(slow, fast, SPLIT_HI * SPLIT_LO)
    cos_fast, sin_fast = phase_table(fast, fast, SPLIT_LO)
    second_matrix = jnp.concatenate(
        [
            jnp.concatenate([cos_fast, -sin_fast], axis=1),
            jnp.concatenate([sin_fast, cos_fast], axis=1),
        ]
    ) * (1.0 / math.sqrt(SPLIT_HI * SPLIT_LO))
    return (first_matrix, cos_turn, sin_turn), (second_matrix, cos_row, sin_row)


def shards(owners, coefficients, batch_weights, claimed, point_index, point_cycle):
    polys, extent, rows_here = coefficients.shape
    length = extent * rows_here * owners
    first_tables, second_tables = transform_tables(extent, rows_here, length)
    chunks = math.gcd(CHUNKS, polys)
    count = polys // chunks
    received = []
    for i in range(chunks):
        sent = first_section(coefficients, first_tables, i * count, count, owners)
        received.append(lax.all_to_all(sent, "coef", split_axis=0, concat_axis=0, tiled=True))

    combined = combine(batch_weights, coefficients)
    combined_here = lax.psum_scatter(
        combined, ("poly", "limb"), scatter_dimension=0, tiled=True
    )
    offsets = jnp.sum(batch_weights[None] * claimed, axis=2)
    offsets_here = lax.psum_scatter(
        offsets, ("poly", "limb"), scatter_dimension=1, tiled=True
    )
    quotient = quotient_section(combined_here, offsets_here, point_index, point_cycle, owners)

    evaluations = None
    for i in range(chunks):
        evaluations = second_section(
            received[i], second_tables, i * count, polys, evaluations
        )
    return (evaluations, quotient)


def solution(mesh):
    placed = (
        P(("parts", "poly", "limb"), None, "coef"),
        P("parts", ("poly", "limb")),
        P(None, "parts", ("poly", "limb")),
        P(("parts", "poly", "limb")),
        P(("parts", "poly", "limb")),
    )
    return jax.shard_map(
        functools.partial(shards, mesh.shape["coef"]),
        mesh=mesh,
        in_specs=placed,
        out_specs=(
            P(None, "coef", ("parts", "poly", "limb"), None, None),
            P(None, ("parts", "poly", "limb"), None, "coef"),
        ),
        check_vma=False,
    )
```

time: 717 us -> 362 us (0.50)
  matrix products: 159 us -> 0 us
  local copies, waits for them, and re-layouts: 180 us -> 24.9 us
  waiting for transfers between devices: 275 us -> 192 us
  Pallas kernels: 0 us -> 73.2 us
  other arithmetic: 58.2 us -> 15.8 us
  blocking collectives: 6.24 us -> 19.7 us
    dot_general x33 -> x0, matrix products: 159 us -> none  [the longest x28 119 us: product(): return jnp.einsum(pattern, matrix, operand, precision=precise)]
    pallas_call x0 -> x10, Pallas kernels: none -> 73.2 us  [the longest x4 43 us: second_section(): pl.pallas_call(second_kernel, grid=(count, per_target // here), in_specs=...]
    reduce_scatter x1, waiting for transfers between devices: 72.2 us -> 0.01 us  [shards(): lax.psum_scatter(combined, ('poly', 'limb'), scatter_dimension=0, tiled=T...]
    another operation x3 -> x1, local copies, waits for them, and re-layouts: 40.3 us -> 0.1 us  [the longest x2 26.8 us: first_section(): return jnp.stack(pieces)]
    all_to_all x4 -> x0, local copies, waits for them, and re-layouts: 38.1 us -> none  [the longest x1 16.4 us: shards(): lax.all_to_all(sectioned, 'coef', split_axis=1, concat_axis=3, tiled=True)]
    another operation x5 -> x4, other arithmetic: 29.6 us -> 0.08 us  [the longest x1 0.06 us: quotient_section(): jnp.stack([turn_real * shift[0] - turn_imag * shift[1], turn_real * shift...]
    slice x5 -> x1, local copies, waits for them, and re-layouts: 23.4 us -> 0.01 us  [quotient_section(): ends_real = jnp.transpose(gathered[:, 0], (1, 0, 2))[:, None]]
    squeeze x4 -> x0, local copies, waits for them, and re-layouts: 21.2 us -> none  [the longest x2 11.1 us: second_section(): shaped[0]]
  transfers between devices with their start and end apart: 4 -> 5, of which waited for: 3 -> 4; matrix products, arithmetic and copies ran while one was open for 40% -> 2% of each run, Pallas kernels for 0% -> 18%
where the time goes in v1:
time: 362 us; the launch traced here: 361 us
  waiting for transfers between devices  192 us (53%)
  Pallas kernels  73.2 us (20%)
  local copies, waits for them, and re-layouts  24.9 us (7%)
  blocking collectives  19.7 us (5%)
  starting transfers between devices  19.5 us (5%)
  other arithmetic  15.8 us (4%)
  between operations  15 us (4%)
    all_to_all x4, waiting for transfers between devices, shards(): lax.all_to_all(sent, 'coef', split_axis=0, concat_axis=0, tiled=True)  192 us
    pallas_call x4, Pallas kernels, second_section(): pl.pallas_call(second_kernel, grid=(count, per_target // here), in_specs=...  43 us
    unnamed x38, local copies, waits for them, and re-layouts  24.5 us
    all_to_all x4, starting transfers between devices, shards(): lax.all_to_all(sent, 'coef', split_axis=0, concat_axis=0, tiled=True)  19.5 us
    pallas_call x4, Pallas kernels, first_section(): pl.pallas_call(first_kernel, grid=(count,), in_specs=[pl.BlockSpec((2 * e...  13.4 us
    all_gather x1, blocking collectives, quotient_section(): gathered = lax.all_gather(ends, 'coef')  13.2 us
    pallas_call x1, Pallas kernels, combine(): pl.pallas_call(combine_kernel, grid=(extent // 8,), in_specs=[pl.BlockSpe...  11.4 us
  transfers between devices with their start and end apart: 5, of which 4 were waited for; matrix products, arithmetic and copies ran while one was open for 2% of the time, Pallas kernels for 18%

profile of v1, /device:TPU:0, one launch (start us, length us, event | category | flops | bytes accessed | tf_op | source)
XLA Modules:
  0.0 360.6 jit_solution(7005543165381630650)
XLA Ops:
  7.2 0.3 fusion.19
  7.5 2.0 fusion.8
  9.5 0.0 copy-start
  9.6 2.8 copy-done
  12.3 3.3 first_section.7
  15.7 0.0 copy-start.7
  15.7 1.7 copy-done.7
  17.4 6.5 %all-to-all-start.3 = ((f32[4,3,2,8,32,128]{5,4,3,2,1,0:T(8,128)}), f32[4,3,2,8,32,128]{5,4,3,2,1,0:T(8,128)}, u32[]{:S(2)}, u32[]{:S(2)}) async-start(f32[4,3,2,8,32,128]{5,4,3,2,1,0:T(8,128)} %copy-done.7), calls=%async_computation.3 | async-start | bytes 6291456 | tf_op jit(solution)/shard_map/all_to_all | solution.py:302
  23.8 2.8 copy-done.1
  26.6 11.4 %combine.1 = f32[16,128,1024]{2,1,0:T(8,128)S(1)} custom-call(f32[16,12]{1,0:T(8,128)S(1)} %copy-done.12, f32[12,128,1024]{2,1,0:T(8,128)S(1)} %copy-done.1), custom_call_target="tpu_custom_call" | custom-call | flops 503316480 | bytes 14680064 | tf_op jit(solution)/shard_map/combine/pallas_call | solution.py:164
  38.1 0.0 copy-start.5
  38.1 3.2 copy-done.5
  41.3 0.0 reduce-scatter.3.cloned.1.call-update
  41.3 0.0 copy-start.2
  41.3 2.8 copy-done.2
  44.1 3.4 first_section.6
  47.5 0.0 copy-start.9
  47.5 1.7 copy-done.9
  49.2 45.4 %all-to-all-done.3.in_ref = f32[4,3,2,8,32,128]{5,4,3,2,1,0:T(8,128)} async-done(((f32[4,3,2,8,32,128]{5,4,3,2,1,0:T(8,128)}), f32[4,3,2,8,32,128]{5,4,3,2,1,0:T(8,128)}, u32[]{:S(2)}, u32[]{:S(2)}) %all-to-all-start.3) | async-done | bytes 3145760 | tf_op jit(solution)/shard_map/all_to_all | solution.py:302
  94.6 4.7 %all-to-all-start.2 = ((f32[4,3,2,8,32,128]{5,4,3,2,1,0:T(8,128)}), f32[4,3,2,8,32,128]{5,4,3,2,1,0:T(8,128)}, u32[]{:S(2)}, u32[]{:S(2)}) async-start(f32[4,3,2,8,32,128]{5,4,3,2,1,0:T(8,128)} %copy-done.9), calls=%async_computation.2 | async-start | bytes 6291456 | tf_op jit(solution)/shard_map/all_to_all | solution.py:302
  99.3 0.0 copy-start.3
  99.3 2.8 copy-done.3
  102.1 3.4 first_section.5
  105.4 0.0 copy-start.8
  105.5 1.7 copy-done.8
  107.1 62.4 %all-to-all-done.2.in_ref = f32[4,3,2,8,32,128]{5,4,3,2,1,0:T(8,128)} async-done(((f32[4,3,2,8,32,128]{5,4,3,2,1,0:T(8,128)}), f32[4,3,2,8,32,128]{5,4,3,2,1,0:T(8,128)}, u32[]{:S(2)}, u32[]{:S(2)}) %all-to-all-start.2) | async-done | bytes 3145760 | tf_op jit(solution)/shard_map/all_to_all | solution.py:302
  169.5 4.7 %all-to-all-start.1 = ((f32[4,3,2,8,32,128]{5,4,3,2,1,0:T(8,128)}), f32[4,3,2,8,32,128]{5,4,3,2,1,0:T(8,128)}, u32[]{:S(2)}, u32[]{:S(2)}) async-start(f32[4,3,2,8,32,128]{5,4,3,2,1,0:T(8,128)} %copy-done.8), calls=%async_computation.1 | async-start | bytes 6291456 | tf_op jit(solution)/shard_map/all_to_all | solution.py:302
  174.2 0.0 copy-start.4
  174.2 2.8 copy-done.4
  177.0 3.4 first_section.4
  180.3 0.0 copy-start.6
  180.3 1.7 copy-done.6
  182.0 62.4 %all-to-all-done.1.in_ref = f32[4,3,2,8,32,128]{5,4,3,2,1,0:T(8,128)} async-done(((f32[4,3,2,8,32,128]{5,4,3,2,1,0:T(8,128)}), f32[4,3,2,8,32,128]{5,4,3,2,1,0:T(8,128)}, u32[]{:S(2)}, u32[]{:S(2)}) %all-to-all-start.1) | async-done | bytes 3145760 | tf_op jit(solution)/shard_map/all_to_all | solution.py:302
  244.5 3.7 %all-to-all-start = ((f32[4,3,2,8,32,128]{5,4,3,2,1,0:T(8,128)}), f32[4,3,2,8,32,128]{5,4,3,2,1,0:T(8,128)S(1)}, u32[]{:S(2)}, u32[]{:S(2)}) async-start(f32[4,3,2,8,32,128]{5,4,3,2,1,0:T(8,128)} %copy-done.6), calls=%async_computation | async-start | bytes 6291456 | tf_op jit(solution)/shard_map/all_to_all | solution.py:302
  248.2 0.1 copy.33
  248.3 0.6 dynamic-slice.8
  249.5 6.5 %all-reduce = f32[2,16]{1,0:T(2,128)S(1)} all-reduce(f32[2,16]{1,0:T(2,128)S(1)} %multiply_reduce_fusion.2), channel_id=4, replica_groups=mesh['parts'=2,'coef'=4,'poly'=2,'limb'=2] {'poly','limb'}, use_global_device_ids=true, to_apply=%region_4.5.clone | all-reduce | flops 32 | bytes 256
  256.1 0.1 dynamic-slice_multiply_fusion
  256.1 0.1 fusion.30
  256.2 0.1 copy.34
  256.3 0.1 fusion.34
  256.4 0.1 copy.35
  256.5 0.1 cosine_multiply_fusion.2
  256.7 0.1 fusion.27
  256.9 0.3 fusion.18
  257.1 0.9 maximum_multiply_fusion.mat_ref
  258.0 1.1 negate_select_fusion.5
  259.1 0.8 pad_maximum_fusion.matrix_ref
  259.9 0.2 sine_multiply_fusion.1
  260.1 0.9 convert_negate_fusion
  261.0 0.9 fusion.7
  261.9 11.4 %second_section.4.rest_0_ = f32[2,32,12,32,128]{4,3,2,1,0:T(8,128)} custom-call(f32[256,256]{1,0:T(8,128)S(1)} %maximum_multiply_fusion.mat_ref, f32[32,128]{1,0:T(8,128)S(1)} %get-tuple-element.35.cos_ref, f32[32,128]{1,0:T(8,128)S(1)} %get-tuple-element.34.sin_ref, f32[4,3,2,8,32,128]{5,4,3,2,1,0:T(8,128)} %all-to-all-done.3.in_ref), custom_call_target="tpu_custom_call" | custom-call | flops 2415919104 | bytes 6291456 | tf_op jit(solution)/shard_map/second_section/pallas_call | solution.py:132
  273.4 11.4 %second_section.5.rest_0_ = f32[2,32,12,32,128]{4,3,2,1,0:T(8,128)} custom-call(f32[256,256]{1,0:T(8,128)S(1)} %maximum_multiply_fusion.mat_ref, f32[32,128]{1,0:T(8,128)S(1)} %get-tuple-element.35.cos_ref, f32[32,128]{1,0:T(8,128)S(1)} %get-tuple-element.34.sin_ref, ...), custom_call_target="tpu_custom_call", output_to_operand_aliasing={{}: (4, {})} | custom-call | flops 2415919104 | bytes 6291456 | tf_op jit(solution)/shard_map/second_section/pallas_call | solution.py:132
  284.8 11.4 %second_section.6.rest_0_ = f32[2,32,12,32,128]{4,3,2,1,0:T(8,128)} custom-call(f32[256,256]{1,0:T(8,128)S(1)} %maximum_multiply_fusion.mat_ref, f32[32,128]{1,0:T(8,128)S(1)} %get-tuple-element.35.cos_ref, f32[32,128]{1,0:T(8,128)S(1)} %get-tuple-element.34.sin_ref, ...), custom_call_target="tpu_custom_call", output_to_operand_aliasing={{}: (4, {})} | custom-call | flops 2415919104 | bytes 6291456 | tf_op jit(solution)/shard_map/second_section/pallas_call | solution.py:132
  296.2 22.2 %all-to-all-done.in_ref = f32[4,3,2,8,32,128]{5,4,3,2,1,0:T(8,128)S(1)} async-done(((f32[4,3,2,8,32,128]{5,4,3,2,1,0:T(8,128)}), f32[4,3,2,8,32,128]{5,4,3,2,1,0:T(8,128)S(1)}, u32[]{:S(2)}, u32[]{:S(2)}) %all-to-all-start) | async-done | bytes 3145760 | tf_op jit(solution)/shard_map/all_to_all | solution.py:302
  318.4 8.8 %second_section.7 = f32[2,32,12,32,128]{4,3,2,1,0:T(8,128)} custom-call(f32[256,256]{1,0:T(8,128)S(1)} %maximum_multiply_fusion.mat_ref, f32[32,128]{1,0:T(8,128)S(1)} %get-tuple-element.35.cos_ref, f32[32,128]{1,0:T(8,128)S(1)} %get-tuple-element.34.sin_ref, f32[4,3,2,8,32,128]{5,4,3,2,1,0:T(8,128)S(1)} %all-to-all-done.in_ref, ...), custom_call_target="tpu_custom_call", output_to_operand_aliasing={{}: (4, {})} | custom-call | flops 2415919104 | bytes 6291456 | tf_op jit(solution)/shard_map/second_section/pallas_call | solution.py:132
  327.1 2.2 multiply_reduce_fusion.1
  329.3 13.2 %all-gather = f32[8,4,128]{2,1,0:T(4,128)S(1)} all-gather(f32[2,4,128]{2,1,0:T(4,128)S(1)} %pad_maximum_fusion.2), channel_id=2, replica_groups=mesh['parts'=2,'coef'=4,'poly'=2,'limb'=2] {'coef'}, dimensions={0}, use_global_device_ids=true | all-gather | bytes 20480 | tf_op jit(solution)/shard_map/all_gather | solution.py:227
  342.5 0.1 scatter-add.4
  342.6 5.6 %subtract_reduce_fusion = (f32[4,128]{1,0:T(4,128)S(1)}, f32[4,128]{1,0:T(4,128)S(1)}) fusion(f32[4,4,128]{2,1,0:T(4,128)S(1)} %bitcast.47, f32[4,4,128]{2,1,0:T(4,128)S(1)} %bitcast.46, s32[4]{0:T(128)S(1)} %copy-done.15, s32[128,4,128]{2,0,1:T(8,128)} %fusion.7, f32[4]{0:T(128)S(1)} %get-tuple-element.31, f32[128,4,128]{2,0,1:T(8,128)} %convert_negate_fusion), kind=kLoop, calls=%fused_computation.3 | loop fusion | flops 3931136 | bytes 544800 | tf_op jit(solution)/shard_map/reduce_sum | solution.py:251
  348.2 0.1 maximum_divide_fusion
  348.3 0.2 copy.36
  348.4 0.1 select_add_fusion.carry_ref
  348.6 5.2 %quotient.1 = f32[2,4,128,1024]{3,2,1,0:T(8,128)} custom-call(f32[4,128,256]{2,1,0:T(8,128)S(1)} %copy-done.11, f32[4,2,128]{2,1,0:T(2,128)S(1)} %pad_maximum_fusion.1.step_ref, f32[4,128,2]{2,1,0:T(8,128)S(1)} %select_add_fusion.carry_ref, f32[4,128,1024]{2,1,0:T(8,128)S(1)} %copy-done.10), custom_call_target="tpu_custom_call" | custom-call | flops 1610612736 | bytes 6291456 | tf_op jit(solution)/shard_map/quotient/pallas_call | solution.py:257
  (41 shorter events, 0.2 us)
Async XLA Ops:
  7.5 8.2 %copy-start.13 = (f32[128,128]{1,0:T(8,128)}, f32[128,128]{1,0:T(8,128)S(1)}, u32[]{:S(2)}) copy-start(f32[128,128]{1,0:T(8,128)S(1)} %get-tuple-element.33) | copy-start | bytes 196612
  9.5 2.8 copy-start
  15.7 1.7 copy-start.7
  17.4 6.5 %copy-start.12 = (f32[16,12]{1,0:T(8,128)S(1)}, f32[16,12]{1,0:T(8,128)}, u32[]{:S(2)}) copy-start(f32[16,12]{1,0:T(8,128)} %weight_ref.1) | copy-start | bytes 2308
  17.4 77.2 %all-to-all-start.3 = ((f32[4,3,2,8,32,128]{5,4,3,2,1,0:T(8,128)}), f32[4,3,2,8,32,128]{5,4,3,2,1,0:T(8,128)}, u32[]{:S(2)}, u32[]{:S(2)}) async-start(f32[4,3,2,8,32,128]{5,4,3,2,1,0:T(8,128)} %copy-done.7), calls=%async_computation.3 | async-start | bytes 6291456 | tf_op jit(solution)/shard_map/all_to_all | solution.py:302
  23.8 303.3 %reduce-scatter.3.cloned.1.call-start = ((), (), s32[]{:S(2)}) async-start(), calls=%async_computation.5 | async-start | bytes 10485760 | tf_op jit(solution)/shard_map/reduce_scatter | solution.py:305
  23.8 2.8 copy-start.1
  38.1 3.2 copy-start.5
  41.3 2.8 copy-start.2
  47.5 1.7 copy-start.9
  94.6 74.9 %all-to-all-start.2 = ((f32[4,3,2,8,32,128]{5,4,3,2,1,0:T(8,128)}), f32[4,3,2,8,32,128]{5,4,3,2,1,0:T(8,128)}, u32[]{:S(2)}, u32[]{:S(2)}) async-start(f32[4,3,2,8,32,128]{5,4,3,2,1,0:T(8,128)} %copy-done.9), calls=%async_computation.2 | async-start | bytes 6291456 | tf_op jit(solution)/shard_map/all_to_all | solution.py:302
  99.3 2.8 copy-start.3
  105.4 1.7 copy-start.8
  169.5 75.0 %all-to-all-start.1 = ((f32[4,3,2,8,32,128]{5,4,3,2,1,0:T(8,128)}), f32[4,3,2,8,32,128]{5,4,3,2,1,0:T(8,128)}, u32[]{:S(2)}, u32[]{:S(2)}) async-start(f32[4,3,2,8,32,128]{5,4,3,2,1,0:T(8,128)} %copy-done.8), calls=%async_computation.1 | async-start | bytes 6291456 | tf_op jit(solution)/shard_map/all_to_all | solution.py:302
  174.2 2.8 copy-start.4
  180.3 1.7 copy-start.6
  182.0 66.2 %copy-start.17 = (u32[32]{0:T(128)S(1)}, u32[32]{0:T(128)}, u32[]{:S(2)}) copy-start(u32[32]{0:T(128)} %constant.151) | copy-start | bytes 388
  182.0 67.5 %copy-start.14 = (f32[2,16,12]{1,0,2:T(2,128)S(1)}, f32[2,16,12]{1,0,2:T(2,128)}, u32[]{:S(2)}) copy-start(f32[2,16,12]{1,0,2:T(2,128)} %param.9) | copy-start | bytes 4612
  182.0 74.1 %copy-start.15 = (s32[4]{0:T(128)S(1)}, s32[4]{0:T(128)}, u32[]{:S(2)}) copy-start(s32[4]{0:T(128)} %param.10) | copy-start | bytes 52
  182.0 74.1 %copy-start.16 = (s32[4]{0:T(128)S(1)}, s32[4]{0:T(128)}, u32[]{:S(2)}) copy-start(s32[4]{0:T(128)} %param.11) | copy-start | bytes 52
  244.5 73.9 %all-to-all-start = ((f32[4,3,2,8,32,128]{5,4,3,2,1,0:T(8,128)}), f32[4,3,2,8,32,128]{5,4,3,2,1,0:T(8,128)S(1)}, u32[]{:S(2)}, u32[]{:S(2)}) async-start(f32[4,3,2,8,32,128]{5,4,3,2,1,0:T(8,128)} %copy-done.6), calls=%async_computation | async-start | bytes 6291456 | tf_op jit(solution)/shard_map/all_to_all | solution.py:302
  327.1 21.4 %copy-start.11 = (f32[4,128,256]{2,1,0:T(8,128)S(1)}, f32[4,128,256]{2,1,0:T(8,128)}, u32[]{:S(2)}) copy-start(f32[4,128,256]{2,1,0:T(8,128)} %pad_maximum_fusion.matrix_ref) | copy-start | bytes 1572868
  327.1 21.4 %copy-start.10 = (f32[4,128,1024]{2,1,0:T(8,128)S(1)}, f32[4,128,1024]{2,1,0:T(8,128)}, u32[]{:S(2)}) copy-start(f32[4,128,1024]{2,1,0:T(8,128)} %reduce-scatter.3.cloned.1.call-done.c_ref) | copy-start | bytes 6291460
Sparse Core Ops, SparseCore 0:
  41.5 72.8 reduce-scatter.2

commit v2 on v1

--- a/solution.py
+++ b/solution.py
@@ -10,7 +10,7 @@
 
 SPLIT_HI = 32
 SPLIT_LO = 128
-CHUNKS = 4
+SHARE = 6
 
 precise = lax.Precision.HIGHEST
 
@@ -61,7 +61,7 @@
         ],
         out_specs=pl.BlockSpec(block, lambda p: (0, p, 0, 0, 0, 0)),
         out_shape=jax.ShapeDtypeStruct(shape, jnp.float32),
-        compiler_params=pltpu.CompilerParams(vmem_limit_bytes=24 << 20),
+        compiler_params=pltpu.CompilerParams(vmem_limit_bytes=60 << 20),
         cost_estimate=cost(size * extent * 12, size * 6),
         name="first_section",
     )(matrix, cos_turn, sin_turn, values)
@@ -170,7 +170,7 @@
         ],
         out_specs=pl.BlockSpec((columns, 8, rows_here), lambda n: (0, n, 0)),
         out_shape=jax.ShapeDtypeStruct((columns, extent, rows_here), jnp.float32),
-        compiler_params=pltpu.CompilerParams(vmem_limit_bytes=16 << 20),
+        compiler_params=pltpu.CompilerParams(vmem_limit_bytes=60 << 20),
         cost_estimate=cost(size * columns * polys * 20, size * 4 * (columns + polys)),
         name="combine",
     )(weights, values)
@@ -294,28 +294,35 @@
     polys, extent, rows_here = coefficients.shape
     length = extent * rows_here * owners
     first_tables, second_tables = transform_tables(extent, rows_here, length)
-    chunks = math.gcd(CHUNKS, polys)
-    count = polys // chunks
-    received = []
-    for i in range(chunks):
-        sent = first_section(coefficients, first_tables, i * count, count, owners)
-        received.append(lax.all_to_all(sent, "coef", split_axis=0, concat_axis=0, tiled=True))
-
-    combined = combine(batch_weights, coefficients)
+    edge = max(1, polys // SHARE)
+    counts = (edge, polys - 2 * edge, edge)
+    starts = (0, edge, polys - edge)
+
+    def opened(i, tables):
+        return first_section(coefficients, tables, starts[i], counts[i], owners)
+
+    def passed(sent):
+        return lax.all_to_all(sent, "coef", split_axis=0, concat_axis=0, tiled=True)
+
+    sent, weights = lax.optimization_barrier((opened(0, first_tables), batch_weights))
+    received = [passed(sent)]
+    combined = combine(weights, coefficients)
     combined_here = lax.psum_scatter(
         combined, ("poly", "limb"), scatter_dimension=0, tiled=True
     )
+    received.append(passed(opened(1, first_tables)))
     offsets = jnp.sum(batch_weights[None] * claimed, axis=2)
     offsets_here = lax.psum_scatter(
         offsets, ("poly", "limb"), scatter_dimension=1, tiled=True
     )
     quotient = quotient_section(combined_here, offsets_here, point_index, point_cycle, owners)
-
-    evaluations = None
-    for i in range(chunks):
-        evaluations = second_section(
-            received[i], second_tables, i * count, polys, evaluations
-        )
+    evaluations = second_section(received[0], second_tables, starts[0], polys, None)
+    matrix, quotient, evaluations = lax.optimization_barrier(
+        (first_tables[0], quotient, evaluations)
+    )
+    received.append(passed(opened(2, (matrix,) + first_tables[1:])))
+    for i in (1, 2):
+        evaluations = second_section(received[i], second_tables, starts[i], polys, evaluations)
     return (evaluations, quotient)
 
 

time: 362 us -> 358 us (0.989)
  blocking collectives: 19.7 us -> 175 us
  waiting for transfers between devices: 192 us -> 52.9 us
  local copies, waits for them, and re-layouts: 24.9 us -> 1.3 us
  Pallas kernels: 73.2 us -> 82.9 us
  starting transfers between devices: 19.5 us -> 15.7 us
    all_gather x1, blocking collectives: 13.2 us -> 169 us  [quotient_section(): gathered = lax.all_gather(ends, 'coef')]
    all_to_all x4 -> x3, waiting for transfers between devices: 192 us -> 52.9 us  [passed(): return lax.all_to_all(sent, 'coef', split_axis=0, concat_axis=0, tiled=True)]
    unnamed x38 -> x14, local copies, waits for them, and re-layouts: 24.5 us -> 0.69 us
    pallas_call x4 -> x3, Pallas kernels: 13.4 us -> 21.2 us  [first_section(): pl.pallas_call(first_kernel, grid=(count,), in_specs=[pl.BlockSpec((2 * e...]
    pallas_call x1, Pallas kernels: 11.4 us -> 15.8 us  [combine(): pl.pallas_call(combine_kernel, grid=(extent // 8,), in_specs=[pl.BlockSpe...]
    all_to_all x4 -> x3, starting transfers between devices: 19.5 us -> 15.7 us  [passed(): return lax.all_to_all(sent, 'coef', split_axis=0, concat_axis=0, tiled=True)]
    pallas_call x4 -> x3, Pallas kernels: 43 us -> 40.6 us  [second_section(): pl.pallas_call(second_kernel, grid=(count, per_target // here), in_specs=...]
  transfers between devices with their start and end apart: 5 -> 4, of which waited for: 4 -> 2; matrix products, arithmetic and copies ran while one was open for 2% -> 3% of each run, Pallas kernels for 18% -> 16%
where the time goes in v2:
time: 358 us; the launch traced here: 357 us
  blocking collectives  175 us (49%)
  Pallas kernels  82.9 us (23%)
  waiting for transfers between devices  52.9 us (15%)
  starting transfers between devices  15.7 us (4%)
  between operations  14.9 us (4%)
  other arithmetic  13.4 us (4%)
    all_gather x1, blocking collectives, quotient_section(): gathered = lax.all_gather(ends, 'coef')  169 us
    all_to_all x3, waiting for transfers between devices, passed(): return lax.all_to_all(sent, 'coef', split_axis=0, concat_axis=0, tiled=True)  52.9 us
    pallas_call x3, Pallas kernels, second_section(): pl.pallas_call(second_kernel, grid=(count, per_target // here), in_specs=...  40.6 us
    pallas_call x3, Pallas kernels, first_section(): pl.pallas_call(first_kernel, grid=(count,), in_specs=[pl.BlockSpec((2 * e...  21.2 us
    pallas_call x1, Pallas kernels, combine(): pl.pallas_call(combine_kernel, grid=(extent // 8,), in_specs=[pl.BlockSpe...  15.8 us
    all_to_all x3, starting transfers between devices, passed(): return lax.all_to_all(sent, 'coef', split_axis=0, concat_axis=0, tiled=True)  15.7 us
  transfers between devices with their start and end apart: 4, of which 2 were waited for; matrix products, arithmetic and copies ran while one was open for 3% of the time, Pallas kernels for 16%

profile of v2, /device:TPU:0, one launch (start us, length us, event | category | flops | bytes accessed | tf_op | source)
XLA Modules:
  0.0 356.6 jit_solution(1627604535675734224)
XLA Ops:
  7.2 0.0 reduce-scatter.3.cloned.1.call-start
  7.2 0.3 fusion.19
  7.5 2.9 fusion.8
  10.4 0.7 maximum_multiply_fusion.1.mat_ref
  11.1 4.5 %first_section.3 = f32[4,2,2,8,32,128]{5,4,3,2,1,0:T(8,128)} custom-call(f32[256,128]{1,0:T(8,128)} %maximum_multiply_fusion.1.mat_ref, f32[128,1024]{1,0:T(8,128)} %get-tuple-element.35.cos_ref, f32[128,1024]{1,0:T(8,128)} %get-tuple-element.34.sin_ref, f32[12,128,1024]{2,1,0:T(8,128)} %x_ref.7), custom_call_target="tpu_custom_call" | custom-call | flops 805306368 | bytes 3145728 | tf_op jit(solution)/shard_map/first_section/pallas_call | solution.py:53
  15.6 15.8 %combine.1 = f32[16,128,1024]{2,1,0:T(8,128)} custom-call(f32[16,12]{1,0:T(8,128)} %weight_ref, f32[12,128,1024]{2,1,0:T(8,128)} %x_ref.7), custom_call_target="tpu_custom_call" | custom-call | flops 503316480 | bytes 14680064 | tf_op jit(solution)/shard_map/combine/pallas_call | solution.py:164
  31.4 0.0 reduce-scatter.3.cloned.1.call-update
  31.4 6.4 %all-to-all-start = ((f32[4,2,2,8,32,128]{5,4,3,2,1,0:T(8,128)}), f32[4,2,2,8,32,128]{5,4,3,2,1,0:T(8,128)S(1)}, u32[]{:S(2)}, u32[]{:S(2)}) async-start(f32[4,2,2,8,32,128]{5,4,3,2,1,0:T(8,128)} %first_section.3), calls=%async_computation.1 | async-start | bytes 4194304 | tf_op jit(solution)/shard_map/all_to_all | solution.py:305
  37.8 12.3 %first_section.5 = f32[4,8,2,8,32,128]{5,4,3,2,1,0:T(8,128)} custom-call(f32[256,128]{1,0:T(8,128)} %maximum_multiply_fusion.1.mat_ref, f32[128,1024]{1,0:T(8,128)} %get-tuple-element.35.cos_ref, f32[128,1024]{1,0:T(8,128)} %get-tuple-element.34.sin_ref, f32[12,128,1024]{2,1,0:T(8,128)} %x_ref.7), custom_call_target="tpu_custom_call" | custom-call | flops 3221225472 | bytes 12582912 | tf_op jit(solution)/shard_map/first_section/pallas_call | solution.py:53
  50.1 0.0 copy-start.1
  50.1 0.0 copy-start.5
  50.1 0.0 copy-start.2
  50.1 0.0 copy-start.3
  50.1 0.0 copy-start.4
  50.1 35.9 %all-to-all-done.in_ref = f32[4,2,2,8,32,128]{5,4,3,2,1,0:T(8,128)S(1)} async-done(((f32[4,2,2,8,32,128]{5,4,3,2,1,0:T(8,128)}), f32[4,2,2,8,32,128]{5,4,3,2,1,0:T(8,128)S(1)}, u32[]{:S(2)}, u32[]{:S(2)}) %all-to-all-start) | async-done | bytes 2097184 | tf_op jit(solution)/shard_map/all_to_all | solution.py:305
  86.0 5.7 %all-to-all-start.2 = ((f32[4,8,2,8,32,128]{5,4,3,2,1,0:T(8,128)}), f32[4,8,2,8,32,128]{5,4,3,2,1,0:T(8,128)}, u32[]{:S(2)}, u32[]{:S(2)}) async-start(f32[4,8,2,8,32,128]{5,4,3,2,1,0:T(8,128)} %first_section.5), calls=%async_computation.3 | async-start | bytes 16777216 | tf_op jit(solution)/shard_map/all_to_all | solution.py:305
  91.7 0.0 copy-done.1
  91.7 0.1 copy.32
  91.8 0.0 copy-done.5
  91.8 0.6 dynamic-slice.8
  93.0 0.0 copy-done.2
  93.0 6.7 %all-reduce = f32[2,16]{1,0:T(2,128)S(1)} all-reduce(f32[2,16]{1,0:T(2,128)S(1)} %multiply_reduce_fusion.2), channel_id=4, replica_groups=mesh['parts'=2,'coef'=4,'poly'=2,'limb'=2] {'poly','limb'}, use_global_device_ids=true, to_apply=%region_4.5.clone | all-reduce | flops 32 | bytes 256
  99.7 0.1 dynamic-slice_multiply_fusion
  99.8 0.0 copy-done.3
  99.8 0.0 copy-done.4
  99.8 0.1 fusion.30
  99.9 0.1 copy.33
  100.0 0.1 fusion.34
  100.1 0.1 copy.34
  100.2 0.1 cosine_multiply_fusion.2
  100.4 0.1 fusion.27
  100.6 0.3 fusion.18
  100.8 1.1 negate_select_fusion.5
  102.0 0.2 sine_multiply_fusion.1
  102.2 0.2 convert_negate_fusion
  102.4 0.2 fusion.7
  102.6 6.1 %second_section.3.rest_0_ = f32[2,32,12,32,128]{4,3,2,1,0:T(8,128)} custom-call(f32[256,256]{1,0:T(8,128)S(1)} %maximum_multiply_fusion.mat_ref, f32[32,128]{1,0:T(8,128)S(1)} %get-tuple-element.45.cos_ref, f32[32,128]{1,0:T(8,128)S(1)} %get-tuple-element.44.sin_ref, f32[4,2,2,8,32,128]{5,4,3,2,1,0:T(8,128)S(1)} %all-to-all-done.in_ref), custom_call_target="tpu_custom_call" | custom-call | flops 1610612736 | bytes 4194304 | tf_op jit(solution)/shard_map/second_section/pallas_call | solution.py:132
  108.7 0.0 reduce-scatter.3.cloned.1.call-done.c_ref
  108.7 0.0 copy-start
  108.7 2.2 multiply_reduce_fusion.1
  110.9 168.8 %all-gather = f32[8,4,128]{2,1,0:T(4,128)S(1)} all-gather(f32[2,4,128]{2,1,0:T(4,128)S(1)} %pad_maximum_fusion.2), channel_id=2, replica_groups=mesh['parts'=2,'coef'=4,'poly'=2,'limb'=2] {'coef'}, dimensions={0}, use_global_device_ids=true | all-gather | bytes 20480 | tf_op jit(solution)/shard_map/all_gather | solution.py:227
  279.7 0.2 scatter-add.4
  280.0 4.6 %subtract_reduce_fusion = (f32[4,128]{1,0:T(4,128)S(1)}, f32[4,128]{1,0:T(4,128)S(1)}) fusion(f32[4,4,128]{2,1,0:T(4,128)S(1)} %bitcast.47, f32[4,4,128]{2,1,0:T(4,128)S(1)} %bitcast.46, s32[4]{0:T(128)S(1)} %copy-done.3, s32[128,4,128]{2,0,1:T(8,128)S(1)} %fusion.7, f32[4]{0:T(128)S(1)} %get-tuple-element.41, f32[128,4,128]{2,0,1:T(8,128)S(1)} %convert_negate_fusion), kind=kLoop, calls=%fused_computation.3 | loop fusion | flops 3931136 | bytes 544800 | tf_op jit(solution)/shard_map/reduce_sum | solution.py:251
  284.5 0.1 maximum_divide_fusion
  284.6 0.2 copy.35
  284.8 0.1 select_add_fusion.carry_ref
  284.9 0.0 copy-done
  284.9 5.3 %quotient.1 = f32[2,4,128,1024]{3,2,1,0:T(8,128)} custom-call(f32[4,128,256]{2,1,0:T(8,128)S(1)} %pad_maximum_fusion.matrix_ref, f32[4,2,128]{2,1,0:T(2,128)S(1)} %pad_maximum_fusion.1.step_ref, f32[4,128,2]{2,1,0:T(8,128)S(1)} %select_add_fusion.carry_ref, f32[4,128,1024]{2,1,0:T(8,128)S(1)} %copy-done), custom_call_target="tpu_custom_call" | custom-call | flops 1610612736 | bytes 6291456 | tf_op jit(solution)/shard_map/quotient/pallas_call | solution.py:257
  290.1 4.4 %first_section.4 = f32[4,2,2,8,32,128]{5,4,3,2,1,0:T(8,128)} custom-call(f32[256,128]{1,0:T(8,128)} %maximum_multiply_fusion.1.mat_ref, f32[128,1024]{1,0:T(8,128)} %get-tuple-element.35.cos_ref, f32[128,1024]{1,0:T(8,128)} %get-tuple-element.34.sin_ref, f32[12,128,1024]{2,1,0:T(8,128)} %x_ref.7), custom_call_target="tpu_custom_call" | custom-call | flops 805306368 | bytes 3145728 | tf_op jit(solution)/shard_map/first_section/pallas_call | solution.py:53
  294.6 0.0 all-to-all-done.2.in_ref
  294.6 3.6 %all-to-all-start.1 = ((f32[4,2,2,8,32,128]{5,4,3,2,1,0:T(8,128)}), f32[4,2,2,8,32,128]{5,4,3,2,1,0:T(8,128)S(1)}, u32[]{:S(2)}, u32[]{:S(2)}) async-start(f32[4,2,2,8,32,128]{5,4,3,2,1,0:T(8,128)} %first_section.4), calls=%async_computation.2 | async-start | bytes 4194304 | tf_op jit(solution)/shard_map/all_to_all | solution.py:305
  298.2 28.4 %second_section.4.rest_0_ = f32[2,32,12,32,128]{4,3,2,1,0:T(8,128)} custom-call(f32[256,256]{1,0:T(8,128)S(1)} %maximum_multiply_fusion.mat_ref, f32[32,128]{1,0:T(8,128)S(1)} %get-tuple-element.45.cos_ref, f32[32,128]{1,0:T(8,128)S(1)} %get-tuple-element.44.sin_ref, ...), custom_call_target="tpu_custom_call", output_to_operand_aliasing={{}: (4, {})} | custom-call | flops 6442450944 | bytes 16777216 | tf_op jit(solution)/shard_map/second_section/pallas_call | solution.py:132
  326.7 17.0 %all-to-all-done.1.in_ref = f32[4,2,2,8,32,128]{5,4,3,2,1,0:T(8,128)S(1)} async-done(((f32[4,2,2,8,32,128]{5,4,3,2,1,0:T(8,128)}), f32[4,2,2,8,32,128]{5,4,3,2,1,0:T(8,128)S(1)}, u32[]{:S(2)}, u32[]{:S(2)}) %all-to-all-start.1) | async-done | bytes 2097184 | tf_op jit(solution)/shard_map/all_to_all | solution.py:305
  343.7 6.1 %second_section.5 = f32[2,32,12,32,128]{4,3,2,1,0:T(8,128)} custom-call(f32[256,256]{1,0:T(8,128)S(1)} %maximum_multiply_fusion.mat_ref, f32[32,128]{1,0:T(8,128)S(1)} %get-tuple-element.45.cos_ref, f32[32,128]{1,0:T(8,128)S(1)} %get-tuple-element.44.sin_ref, f32[4,2,2,8,32,128]{5,4,3,2,1,0:T(8,128)S(1)} %all-to-all-done.1.in_ref, ...), custom_call_target="tpu_custom_call", output_to_operand_aliasing={{}: (4, {})} | custom-call | flops 1610612736 | bytes 4194304 | tf_op jit(solution)/shard_map/second_section/pallas_call | solution.py:132
  (24 shorter events, 0.2 us)
Async XLA Ops:
  7.2 101.6 %reduce-scatter.3.cloned.1.call-start = ((), (), s32[]{:S(2)}) async-start(), calls=%async_computation.4 | async-start | bytes 10485760 | tf_op jit(solution)/shard_map/reduce_scatter | solution.py:310
  31.4 54.5 %all-to-all-start = ((f32[4,2,2,8,32,128]{5,4,3,2,1,0:T(8,128)}), f32[4,2,2,8,32,128]{5,4,3,2,1,0:T(8,128)S(1)}, u32[]{:S(2)}, u32[]{:S(2)}) async-start(f32[4,2,2,8,32,128]{5,4,3,2,1,0:T(8,128)} %first_section.3), calls=%async_computation.1 | async-start | bytes 4194304 | tf_op jit(solution)/shard_map/all_to_all | solution.py:305
  50.1 41.6 %copy-start.1 = (f32[16,12]{1,0:T(8,128)S(1)}, f32[16,12]{1,0:T(8,128)}, u32[]{:S(2)}) copy-start(f32[16,12]{1,0:T(8,128)} %weight_ref) | copy-start | bytes 2308
  50.1 41.7 %copy-start.5 = (u32[32]{0:T(128)S(1)}, u32[32]{0:T(128)}, u32[]{:S(2)}) copy-start(u32[32]{0:T(128)} %constant.151) | copy-start | bytes 388
  50.1 42.9 %copy-start.2 = (f32[2,16,12]{1,0,2:T(2,128)S(1)}, f32[2,16,12]{1,0,2:T(2,128)}, u32[]{:S(2)}) copy-start(f32[2,16,12]{1,0,2:T(2,128)} %param.9) | copy-start | bytes 4612
  50.1 49.7 %copy-start.3 = (s32[4]{0:T(128)S(1)}, s32[4]{0:T(128)}, u32[]{:S(2)}) copy-start(s32[4]{0:T(128)} %param.10) | copy-start | bytes 52
  50.1 49.7 %copy-start.4 = (s32[4]{0:T(128)S(1)}, s32[4]{0:T(128)}, u32[]{:S(2)}) copy-start(s32[4]{0:T(128)} %param.11) | copy-start | bytes 52
  86.0 208.6 %all-to-all-start.2 = ((f32[4,8,2,8,32,128]{5,4,3,2,1,0:T(8,128)}), f32[4,8,2,8,32,128]{5,4,3,2,1,0:T(8,128)}, u32[]{:S(2)}, u32[]{:S(2)}) async-start(f32[4,8,2,8,32,128]{5,4,3,2,1,0:T(8,128)} %first_section.5), calls=%async_computation.3 | async-start | bytes 16777216 | tf_op jit(solution)/shard_map/all_to_all | solution.py:305
  108.7 176.2 %copy-start = (f32[4,128,1024]{2,1,0:T(8,128)S(1)}, f32[4,128,1024]{2,1,0:T(8,128)}, u32[]{:S(2)}) copy-start(f32[4,128,1024]{2,1,0:T(8,128)} %reduce-scatter.3.cloned.1.call-done.c_ref) | copy-start | bytes 6291460
  294.6 49.1 %all-to-all-start.1 = ((f32[4,2,2,8,32,128]{5,4,3,2,1,0:T(8,128)}), f32[4,2,2,8,32,128]{5,4,3,2,1,0:T(8,128)S(1)}, u32[]{:S(2)}, u32[]{:S(2)}) async-start(f32[4,2,2,8,32,128]{5,4,3,2,1,0:T(8,128)} %first_section.4), calls=%async_computation.2 | async-start | bytes 4194304 | tf_op jit(solution)/shard_map/all_to_all | solution.py:305
Sparse Core Ops, SparseCore 0:
  31.6 74.2 reduce-scatter.2

commit v3 on v2

--- a/solution.py
+++ b/solution.py
@@ -7,6 +7,7 @@
 from jax.experimental import pallas as pl
 from jax.experimental.pallas import tpu as pltpu
 from jax.sharding import PartitionSpec as P
+
 
 SPLIT_HI = 32
 SPLIT_LO = 128
@@ -145,8 +146,9 @@
     )(*operands)
 
 
-def combine_kernel(weight_ref, x_ref, out_ref):
+def combine_kernel(weight_ref, x_ref, *out_refs):
     columns, polys = weight_ref.shape
+    each = columns // len(out_refs)
     for g in range(x_ref.shape[2] // SPLIT_LO):
         cols = slice(g * SPLIT_LO, (g + 1) * SPLIT_LO)
         rows = [x_ref[p, :, cols] for p in range(polys)]
@@ -154,12 +156,13 @@
             total = rows[0] * weight_ref[j, 0]
             for p in range(1, polys):
                 total = total + rows[p] * weight_ref[j, p]
-            out_ref[j, :, cols] = total
-
-
-def combine(weights, values):
+            out_refs[j // each][j % each, :, cols] = total
+
+
+def combine(weights, values, targets):
     polys, extent, rows_here = values.shape
     columns = weights.shape[0]
+    each = columns // targets
     size = extent * rows_here
     return pl.pallas_call(
         combine_kernel,
@@ -168,12 +171,28 @@
             pl.BlockSpec(memory_space=pltpu.SMEM),
             pl.BlockSpec((polys, 8, rows_here), lambda n: (0, n, 0)),
         ],
-        out_specs=pl.BlockSpec((columns, 8, rows_here), lambda n: (0, n, 0)),
-        out_shape=jax.ShapeDtypeStruct((columns, extent, rows_here), jnp.float32),
+        out_specs=[pl.BlockSpec((each, 8, rows_here), lambda n: (0, n, 0))] * targets,
+        out_shape=[jax.ShapeDtypeStruct((each, extent, rows_here), jnp.float32)] * targets,
         compiler_params=pltpu.CompilerParams(vmem_limit_bytes=60 << 20),
         cost_estimate=cost(size * columns * polys * 20, size * 4 * (columns + polys)),
         name="combine",
     )(weights, values)
+
+
+def column_sums(weights, values):
+    axes = ("poly", "limb")
+    group = lax.axis_size(axes)
+    each = weights.shape[0] // group
+    me = lax.axis_index(axes)
+    turned = lax.dynamic_slice_in_dim(
+        jnp.concatenate([weights, weights]), me * each, weights.shape[0], axis=0
+    )
+    parts = combine(turned, values, group)
+    total = parts[0]
+    for step in range(1, group):
+        order = [(i, (i + step) % group) for i in range(group)]
+        total = total + lax.ppermute(parts[step], axes, order)
+    return total
 
 
 def powers(exponents, point_index, log_radius, length):
@@ -185,7 +204,7 @@
 
 
 def quotient_kernel(matrix_ref, step_ref, carry_ref, c_ref, out_ref):
-    rows, width = c_ref.shape[1:]
+    _, width = c_ref.shape[1:]
     lanes = step_ref.shape[2]
     step_real, step_imag = step_ref[0, 0:1], step_ref[0, 1:2]
     carry = carry_ref[0]
@@ -201,7 +220,7 @@
         carry_real, carry_imag = real[:, lanes - 1 :], imag[:, lanes - 1 :]
 
 
-def quotient_section(combined, offsets, point_index, point_cycle, owners):
+def quotient_section(combined, offsets, point_index, point_cycle, owners, sent):
     columns, extent, rows_here = combined.shape
     length = extent * rows_here * owners
     lanes = SPLIT_LO
@@ -224,7 +243,9 @@
             -jnp.sum(combined * end_imag[:, None, :], axis=2),
         ]
     )
+    ends, sent = lax.optimization_barrier((ends, sent))
     gathered = lax.all_gather(ends, "coef")
+    gathered, sent = lax.optimization_barrier((gathered, sent))
     me = lax.axis_index("coef")
     shift = offsets * math.sqrt(length)
     turn_real, turn_imag = power(jnp.full((), rows_here, jnp.int32))
@@ -254,7 +275,7 @@
     starts = ((row == 0) & (me == 0))[None, :, None]
     carry = carry + jnp.where(starts, shift.T[:, None, :], 0.0)
     size = columns * extent * rows_here
-    return pl.pallas_call(
+    call = pl.pallas_call(
         quotient_kernel,
         grid=(columns,),
         in_specs=[
@@ -268,7 +289,8 @@
         compiler_params=pltpu.CompilerParams(vmem_limit_bytes=16 << 20),
         cost_estimate=cost(size * 4 * lanes * 6, size * 12),
         name="quotient",
-    )(matrix, step, carry, combined)
+    )
+    return call(matrix, step, carry, combined), sent
 
 
 def transform_tables(extent, rows_here, length):
@@ -298,31 +320,28 @@
     counts = (edge, polys - 2 * edge, edge)
     starts = (0, edge, polys - edge)
 
-    def opened(i, tables):
-        return first_section(coefficients, tables, starts[i], counts[i], owners)
+    def opened(i):
+        return first_section(coefficients, first_tables, starts[i], counts[i], owners)
 
     def passed(sent):
         return lax.all_to_all(sent, "coef", split_axis=0, concat_axis=0, tiled=True)
 
-    sent, weights = lax.optimization_barrier((opened(0, first_tables), batch_weights))
-    received = [passed(sent)]
-    combined = combine(weights, coefficients)
-    combined_here = lax.psum_scatter(
-        combined, ("poly", "limb"), scatter_dimension=0, tiled=True
-    )
-    received.append(passed(opened(1, first_tables)))
+    received = [passed(opened(0))]
+    combined_here = column_sums(batch_weights, coefficients)
+    received.append(passed(opened(1)))
     offsets = jnp.sum(batch_weights[None] * claimed, axis=2)
     offsets_here = lax.psum_scatter(
         offsets, ("poly", "limb"), scatter_dimension=1, tiled=True
     )
-    quotient = quotient_section(combined_here, offsets_here, point_index, point_cycle, owners)
+    quotient, sent = quotient_section(
+        combined_here, offsets_here, point_index, point_cycle, owners, opened(2)
+    )
+    received.append(passed(sent))
     evaluations = second_section(received[0], second_tables, starts[0], polys, None)
-    matrix, quotient, evaluations = lax.optimization_barrier(
-        (first_tables[0], quotient, evaluations)
-    )
-    received.append(passed(opened(2, (matrix,) + first_tables[1:])))
     for i in (1, 2):
-        evaluations = second_section(received[i], second_tables, starts[i], polys, evaluations)
+        evaluations = second_section(
+            received[i], second_tables, starts[i], polys, evaluations
+        )
     return (evaluations, quotient)
 
 

time: 358 us -> 320 us (0.89)
  blocking collectives: 175 us -> 158 us
  waiting for transfers between devices: 52.9 us -> 36.2 us
  between operations: 14.9 us -> 1.49 us
    all_gather x1, blocking collectives: 169 us -> 66.9 us  [quotient_section(): gathered = lax.all_gather(ends, 'coef')]
    unnamed x1, blocking collectives: 6.7 us -> 91.3 us
    all_to_all x3, waiting for transfers between devices: 52.9 us -> 36.2 us  [passed(): return lax.all_to_all(sent, 'coef', split_axis=0, concat_axis=0, tiled=True)]
  transfers between devices with their start and end apart: 4 -> 6, of which waited for: 2 -> 1; matrix products, arithmetic and copies ran while one was open for 3% -> 4% of each run, Pallas kernels for 16% -> 22%
where the time goes in v3:
time: 320 us; the launch traced here: 318 us
  blocking collectives  158 us (49%)
  Pallas kernels  83.8 us (26%)
  waiting for transfers between devices  36.2 us (11%)
  starting transfers between devices  18.2 us (6%)
  other arithmetic  16 us (5%)
  local copies, waits for them, and re-layouts  3.94 us (1%)
    unnamed x1, blocking collectives  91.3 us
    all_gather x1, blocking collectives, quotient_section(): gathered = lax.all_gather(ends, 'coef')  66.9 us
    pallas_call x3, Pallas kernels, second_section(): pl.pallas_call(second_kernel, grid=(count, per_target // here), in_specs=...  42.5 us
    all_to_all x3, waiting for transfers between devices, passed(): return lax.all_to_all(sent, 'coef', split_axis=0, concat_axis=0, tiled=True)  36.2 us
    pallas_call x3, Pallas kernels, first_section(): pl.pallas_call(first_kernel, grid=(count,), in_specs=[pl.BlockSpec((2 * e...  20.9 us
    all_to_all x3, starting transfers between devices, passed(): return lax.all_to_all(sent, 'coef', split_axis=0, concat_axis=0, tiled=True)  16.4 us
    pallas_call x1, Pallas kernels, combine(): pl.pallas_call(combine_kernel, grid=(extent // 8,), in_specs=[pl.BlockSpe...  15.1 us
  transfers between devices with their start and end apart: 6, of which 1 were waited for; matrix products, arithmetic and copies ran while one was open for 4% of the time, Pallas kernels for 22%

profile of v3, /device:TPU:0, one launch (start us, length us, event | category | flops | bytes accessed | tf_op | source)
XLA Modules:
  0.0 317.9 jit_solution(14753021586353687016)
XLA Ops:
  0.6 0.3 fusion.19
  0.9 2.9 fusion.8
  3.9 0.7 maximum_multiply_fusion.1.mat_ref
  4.5 4.5 %first_section.5 = f32[4,2,2,8,32,128]{5,4,3,2,1,0:T(8,128)} custom-call(f32[256,128]{1,0:T(8,128)} %maximum_multiply_fusion.1.mat_ref, f32[128,1024]{1,0:T(8,128)} %get-tuple-element.42.cos_ref, f32[128,1024]{1,0:T(8,128)} %get-tuple-element.41.sin_ref, f32[12,128,1024]{2,1,0:T(8,128)} %x_ref.7), custom_call_target="tpu_custom_call" | custom-call | flops 805306368 | bytes 3145728 | tf_op jit(solution)/shard_map/first_section/pallas_call | solution.py:54
  9.0 6.3 %all-to-all-start.2 = ((f32[4,2,2,8,32,128]{5,4,3,2,1,0:T(8,128)}), f32[4,2,2,8,32,128]{5,4,3,2,1,0:T(8,128)S(1)}, u32[]{:S(2)}, u32[]{:S(2)}) async-start(f32[4,2,2,8,32,128]{5,4,3,2,1,0:T(8,128)} %first_section.5), calls=%async_computation.2 | async-start | bytes 4194304 | tf_op jit(solution)/shard_map/all_to_all | solution.py:327
  15.3 12.0 %first_section.4 = f32[4,8,2,8,32,128]{5,4,3,2,1,0:T(8,128)} custom-call(f32[256,128]{1,0:T(8,128)} %maximum_multiply_fusion.1.mat_ref, f32[128,1024]{1,0:T(8,128)} %get-tuple-element.42.cos_ref, f32[128,1024]{1,0:T(8,128)} %get-tuple-element.41.sin_ref, f32[12,128,1024]{2,1,0:T(8,128)} %x_ref.7), custom_call_target="tpu_custom_call" | custom-call | flops 3221225472 | bytes 12582912 | tf_op jit(solution)/shard_map/first_section/pallas_call | solution.py:54
  27.3 0.0 copy-start.3
  27.3 36.2 %all-to-all-done.2.in_ref = f32[4,2,2,8,32,128]{5,4,3,2,1,0:T(8,128)S(1)} async-done(((f32[4,2,2,8,32,128]{5,4,3,2,1,0:T(8,128)}), f32[4,2,2,8,32,128]{5,4,3,2,1,0:T(8,128)S(1)}, u32[]{:S(2)}, u32[]{:S(2)}) %all-to-all-start.2) | async-done | bytes 2097184 | tf_op jit(solution)/shard_map/all_to_all | solution.py:327
  63.5 0.0 copy-start
  63.5 1.4 copy-done
  64.9 5.6 %all-to-all-start.1 = ((f32[4,8,2,8,32,128]{5,4,3,2,1,0:T(8,128)}), f32[4,8,2,8,32,128]{5,4,3,2,1,0:T(8,128)}, u32[]{:S(2)}, u32[]{:S(2)}) async-start(f32[4,8,2,8,32,128]{5,4,3,2,1,0:T(8,128)} %first_section.4), calls=%async_computation.1 | async-start | bytes 16777216 | tf_op jit(solution)/shard_map/all_to_all | solution.py:327
  70.6 0.0 copy-done.3
  70.6 0.6 fusion.27.weight_ref
  71.2 0.0 copy-start.7
  71.2 0.0 copy-start.4
  71.2 15.1 %combine.1 = (f32[4,128,1024]{2,1,0:T(8,128)}, f32[4,128,1024]{2,1,0:T(8,128)}, f32[4,128,1024]{2,1,0:T(8,128)}, f32[4,128,1024]{2,1,0:T(8,128)}) custom-call(f32[16,12]{1,0:T(8,128)} %fusion.27.weight_ref, f32[12,128,1024]{2,1,0:T(8,128)} %x_ref.7), custom_call_target="tpu_custom_call" | custom-call | flops 503316480 | bytes 14680064 | tf_op jit(solution)/shard_map/combine/pallas_call | solution.py:167
  86.3 0.2 collective-permute-start.2
  86.5 1.3 collective-permute-start.1
  87.8 0.2 collective-permute-start
  88.0 0.1 copy.32
  88.1 0.0 copy-done.7
  88.1 0.6 dynamic-slice.8
  89.2 0.0 copy-done.4
  89.2 91.3 %all-reduce = f32[2,16]{1,0:T(2,128)S(1)} all-reduce(f32[2,16]{1,0:T(2,128)S(1)} %multiply_reduce_fusion.2), channel_id=3, replica_groups=mesh['parts'=2,'coef'=4,'poly'=2,'limb'=2] {'poly','limb'}, use_global_device_ids=true, to_apply=%region_3.4.clone | all-reduce | flops 32 | bytes 256
  180.6 0.0 copy-start.5
  180.6 0.0 copy-start.6
  180.6 4.5 %first_section.3 = f32[4,2,2,8,32,128]{5,4,3,2,1,0:T(8,128)} custom-call(f32[256,128]{1,0:T(8,128)} %maximum_multiply_fusion.1.mat_ref, f32[128,1024]{1,0:T(8,128)} %get-tuple-element.42.cos_ref, f32[128,1024]{1,0:T(8,128)} %get-tuple-element.41.sin_ref, f32[12,128,1024]{2,1,0:T(8,128)} %x_ref.7), custom_call_target="tpu_custom_call" | custom-call | flops 805306368 | bytes 3145728 | tf_op jit(solution)/shard_map/first_section/pallas_call | solution.py:54
  185.1 0.1 dynamic-slice_multiply_fusion
  185.1 0.1 fusion.35
  185.2 0.0 copy-done.5
  185.2 0.0 copy-done.6
  185.2 0.1 fusion.31
  185.3 0.1 cosine_multiply_fusion.2
  185.5 0.1 fusion.28
  185.6 0.3 fusion.18
  186.0 0.2 sine_multiply_fusion.1
  186.2 0.0 collective-permute-done.2
  186.2 0.0 copy-start.2
  186.2 0.0 collective-permute-done.1
  186.2 0.0 collective-permute-done
  186.2 1.3 copy-done.2
  187.5 4.1 %multiply_reduce_fusion.1 = (f32[4,128]{1,0:T(4,128)S(1)}, f32[4,128]{1,0:T(4,128)S(1)}, f32[4,128,1024]{2,1,0:T(8,128)S(1)}) fusion(f32[4,1024]{1,0:T(4,128)S(1)} %get-tuple-element.40, f32[4,1024]{1,0:T(4,128)S(1)} %get-tuple-element.39, f32[4,128,1024]{2,1,0:T(8,128)} %copy-done.2, f32[4,128,1024]{2,1,0:T(8,128)} %collective-permute-done.1, ...), kind=kLoop, calls=%fused_computation.1 | loop fusion | flops 3668992 | bytes 10522624 | tf_op jit(solution)/shard_map/reduce_sum | solution.py:242
  191.7 66.9 %all-gather = f32[8,4,128]{2,1,0:T(4,128)S(1)} all-gather(f32[2,4,128]{2,1,0:T(4,128)S(1)} %pad_maximum_fusion.1), channel_id=2, replica_groups=mesh['parts'=2,'coef'=4,'poly'=2,'limb'=2] {'coef'}, dimensions={0}, use_global_device_ids=true | all-gather | bytes 20480 | tf_op jit(solution)/shard_map/all_gather | solution.py:247
  258.6 0.0 all-to-all-done.1.in_ref
  258.6 4.5 %all-to-all-start = ((f32[4,2,2,8,32,128]{5,4,3,2,1,0:T(8,128)}), f32[4,2,2,8,32,128]{5,4,3,2,1,0:T(8,128)}, u32[]{:S(2)}, u32[]{:S(2)}) async-start(f32[4,2,2,8,32,128]{5,4,3,2,1,0:T(8,128)} %first_section.3), calls=%async_computation | async-start | bytes 4194304 | tf_op jit(solution)/shard_map/all_to_all | solution.py:327
  263.1 0.1 copy.33
  263.2 0.1 copy.34
  263.3 1.1 negate_select_fusion.5
  264.4 0.2 fusion.7
  264.6 0.2 convert_negate_fusion
  264.8 0.2 scatter-add.4
  265.1 4.6 %subtract_reduce_fusion = (f32[4,128]{1,0:T(4,128)S(1)}, f32[4,128]{1,0:T(4,128)S(1)}) fusion(f32[4,4,128]{2,1,0:T(4,128)S(1)} %bitcast.47, f32[4,4,128]{2,1,0:T(4,128)S(1)} %bitcast.46, s32[4]{0:T(128)S(1)} %copy-done.5, s32[128,4,128]{2,0,1:T(8,128)S(1)} %fusion.7, f32[4]{0:T(128)S(1)} %get-tuple-element.48, f32[128,4,128]{2,0,1:T(8,128)S(1)} %convert_negate_fusion), kind=kLoop, calls=%fused_computation.4 | loop fusion | flops 3931136 | bytes 544800 | tf_op jit(solution)/shard_map/reduce_sum | solution.py:272
  269.7 0.1 maximum_divide_fusion
  269.8 0.2 copy.35
  269.9 0.1 select_add_fusion.carry_ref
  270.0 0.0 copy-start.1
  270.1 5.3 %quotient.1 = f32[2,4,128,1024]{3,2,1,0:T(8,128)} custom-call(f32[4,128,256]{2,1,0:T(8,128)S(1)} %pad_maximum_fusion.matrix_ref, f32[4,2,128]{2,1,0:T(2,128)S(1)} %pad_maximum_fusion.2.step_ref, f32[4,128,2]{2,1,0:T(8,128)S(1)} %select_add_fusion.carry_ref, f32[4,128,1024]{2,1,0:T(8,128)S(1)} %get-tuple-element.34.c_ref), custom_call_target="tpu_custom_call" | custom-call | flops 1610612736 | bytes 6291456 | tf_op jit(solution)/shard_map/quotient/pallas_call | solution.py:293
  275.3 0.0 copy-done.1
  275.3 6.1 %second_section.3.rest_0_ = f32[2,32,12,32,128]{4,3,2,1,0:T(8,128)} custom-call(f32[256,256]{1,0:T(8,128)S(1)} %maximum_multiply_fusion.mat_ref, f32[32,128]{1,0:T(8,128)S(1)} %get-tuple-element.54.cos_ref, f32[32,128]{1,0:T(8,128)S(1)} %get-tuple-element.53.sin_ref, f32[4,2,2,8,32,128]{5,4,3,2,1,0:T(8,128)S(1)} %copy-done.1), custom_call_target="tpu_custom_call" | custom-call | flops 1610612736 | bytes 4194304 | tf_op jit(solution)/shard_map/second_section/pallas_call | solution.py:133
  281.4 28.4 %second_section.4.rest_0_ = f32[2,32,12,32,128]{4,3,2,1,0:T(8,128)} custom-call(f32[256,256]{1,0:T(8,128)S(1)} %maximum_multiply_fusion.mat_ref, f32[32,128]{1,0:T(8,128)S(1)} %get-tuple-element.54.cos_ref, f32[32,128]{1,0:T(8,128)S(1)} %get-tuple-element.53.sin_ref, ...), custom_call_target="tpu_custom_call", output_to_operand_aliasing={{}: (4, {})} | custom-call | flops 6442450944 | bytes 16777216 | tf_op jit(solution)/shard_map/second_section/pallas_call | solution.py:133
  309.8 0.0 all-to-all-done.in_ref
  309.8 8.0 %second_section.5 = f32[2,32,12,32,128]{4,3,2,1,0:T(8,128)} custom-call(f32[256,256]{1,0:T(8,128)S(1)} %maximum_multiply_fusion.mat_ref, f32[32,128]{1,0:T(8,128)S(1)} %get-tuple-element.54.cos_ref, f32[32,128]{1,0:T(8,128)S(1)} %get-tuple-element.53.sin_ref, f32[4,2,2,8,32,128]{5,4,3,2,1,0:T(8,128)} %all-to-all-done.in_ref, ...), custom_call_target="tpu_custom_call", output_to_operand_aliasing={{}: (4, {})} | custom-call | flops 1610612736 | bytes 4194304 | tf_op jit(solution)/shard_map/second_section/pallas_call | solution.py:133
  (23 shorter events, 0.2 us)
Async XLA Ops:
  9.0 54.5 %all-to-all-start.2 = ((f32[4,2,2,8,32,128]{5,4,3,2,1,0:T(8,128)}), f32[4,2,2,8,32,128]{5,4,3,2,1,0:T(8,128)S(1)}, u32[]{:S(2)}, u32[]{:S(2)}) async-start(f32[4,2,2,8,32,128]{5,4,3,2,1,0:T(8,128)} %first_section.5), calls=%async_computation.2 | async-start | bytes 4194304 | tf_op jit(solution)/shard_map/all_to_all | solution.py:327
  27.3 43.2 %copy-start.3 = (f32[16,12]{1,0:T(8,128)S(1)}, f32[16,12]{1,0:T(8,128)}, u32[]{:S(2)}) copy-start(f32[16,12]{1,0:T(8,128)} %param.8) | copy-start | bytes 2308
  63.5 1.4 copy-start
  64.9 193.7 %all-to-all-start.1 = ((f32[4,8,2,8,32,128]{5,4,3,2,1,0:T(8,128)}), f32[4,8,2,8,32,128]{5,4,3,2,1,0:T(8,128)}, u32[]{:S(2)}, u32[]{:S(2)}) async-start(f32[4,8,2,8,32,128]{5,4,3,2,1,0:T(8,128)} %first_section.4), calls=%async_computation.1 | async-start | bytes 16777216 | tf_op jit(solution)/shard_map/all_to_all | solution.py:327
  71.2 16.9 %copy-start.7 = (u32[32]{0:T(128)S(1)}, u32[32]{0:T(128)}, u32[]{:S(2)}) copy-start(u32[32]{0:T(128)} %constant.162) | copy-start | bytes 388
  71.2 18.0 %copy-start.4 = (f32[2,16,12]{1,0,2:T(2,128)S(1)}, f32[2,16,12]{1,0,2:T(2,128)}, u32[]{:S(2)}) copy-start(f32[2,16,12]{1,0,2:T(2,128)} %param.9) | copy-start | bytes 4612
  86.3 99.9 %collective-permute-start.2 = (f32[4,128,1024]{2,1,0:T(8,128)}, f32[4,128,1024]{2,1,0:T(8,128)S(1)}, u32[]{:S(2)}, u32[]{:S(2)}) collective-permute-start(f32[4,128,1024]{2,1,0:T(8,128)} %get-tuple-element.25), channel_id=1, source_target_pairs={{0,3},{1,0},{2,1},{3,2},{4,7},{5,4},{6,5},{7,6},{8,11},{9,8},{10,9... | collective-permute-start | bytes 6291464 | tf_op jit(solution)/shard_map/ppermute | solution.py:194
  86.5 99.7 %collective-permute-start.1 = (f32[4,128,1024]{2,1,0:T(8,128)}, f32[4,128,1024]{2,1,0:T(8,128)}, u32[]{:S(2)}, u32[]{:S(2)}) collective-permute-start(f32[4,128,1024]{2,1,0:T(8,128)} %get-tuple-element.24), channel_id=1, source_target_pairs={{0,2},{1,3},{2,0},{3,1},{4,6},{5,7},{6,4},{7,5},{8,10},{9,11},{10,... | collective-permute-start | bytes 6291464 | tf_op jit(solution)/shard_map/ppermute | solution.py:194
  87.8 98.4 %collective-permute-start = (f32[4,128,1024]{2,1,0:T(8,128)}, f32[4,128,1024]{2,1,0:T(8,128)}, u32[]{:S(2)}, u32[]{:S(2)}) collective-permute-start(f32[4,128,1024]{2,1,0:T(8,128)} %get-tuple-element.23), channel_id=1, source_target_pairs={{0,1},{1,2},{2,3},{3,0},{4,5},{5,6},{6,7},{7,4},{8,9},{9,10},{10,1... | collective-permute-start | bytes 6291464 | tf_op jit(solution)/shard_map/ppermute | solution.py:194
  180.6 4.7 %copy-start.5 = (s32[4]{0:T(128)S(1)}, s32[4]{0:T(128)}, u32[]{:S(2)}) copy-start(s32[4]{0:T(128)} %param.10) | copy-start | bytes 52
  180.6 4.7 %copy-start.6 = (s32[4]{0:T(128)S(1)}, s32[4]{0:T(128)}, u32[]{:S(2)}) copy-start(s32[4]{0:T(128)} %param.11) | copy-start | bytes 52
  186.2 1.3 copy-start.2
  258.6 51.2 %all-to-all-start = ((f32[4,2,2,8,32,128]{5,4,3,2,1,0:T(8,128)}), f32[4,2,2,8,32,128]{5,4,3,2,1,0:T(8,128)}, u32[]{:S(2)}, u32[]{:S(2)}) async-start(f32[4,2,2,8,32,128]{5,4,3,2,1,0:T(8,128)} %first_section.3), calls=%async_computation | async-start | bytes 4194304 | tf_op jit(solution)/shard_map/all_to_all | solution.py:327
  270.0 5.3 %copy-start.1 = (f32[4,2,2,8,32,128]{5,4,3,2,1,0:T(8,128)S(1)}, f32[4,2,2,8,32,128]{5,4,3,2,1,0:T(8,128)}, u32[]{:S(2)}) copy-start(f32[4,2,2,8,32,128]{5,4,3,2,1,0:T(8,128)} %copy-done) | copy-start | bytes 6291460

commit v4 on v3

--- a/solution.py
+++ b/solution.py
@@ -220,7 +220,18 @@
         carry_real, carry_imag = real[:, lanes - 1 :], imag[:, lanes - 1 :]
 
 
-def quotient_section(combined, offsets, point_index, point_cycle, owners, sent):
+def shared(ends, owners):
+    me = lax.axis_index("coef")
+    if owners > 8:
+        return lax.all_gather(ends, "coef"), jnp.arange(owners, dtype=jnp.int32)
+    arrived = [ends]
+    for step in range(1, owners):
+        order = [(i, (i + step) % owners) for i in range(owners)]
+        arrived.append(lax.ppermute(ends, "coef", order))
+    return jnp.stack(arrived), (me - jnp.arange(owners, dtype=jnp.int32)) % owners
+
+
+def quotient_section(combined, offsets, point_index, point_cycle, owners):
     columns, extent, rows_here = combined.shape
     length = extent * rows_here * owners
     lanes = SPLIT_LO
@@ -243,10 +254,8 @@
             -jnp.sum(combined * end_imag[:, None, :], axis=2),
         ]
     )
-    ends, sent = lax.optimization_barrier((ends, sent))
-    gathered = lax.all_gather(ends, "coef")
-    gathered, sent = lax.optimization_barrier((gathered, sent))
     me = lax.axis_index("coef")
+    gathered, owner = shared(ends, owners)
     shift = offsets * math.sqrt(length)
     turn_real, turn_imag = power(jnp.full((), rows_here, jnp.int32))
     first = jnp.stack(
@@ -255,9 +264,11 @@
             turn_real * shift[1] + turn_imag * shift[0],
         ]
     )
-    gathered = gathered.at[0, :, :, 0].add(first)
     row = jnp.arange(extent, dtype=jnp.int32)
-    owner = jnp.arange(owners, dtype=jnp.int32)
+    opening = (owner[:, None] == 0) & (row[None, :] == 0)
+    gathered = gathered + jnp.where(
+        opening[:, None, None, :], first[None, :, :, None], 0.0
+    )
     segments = extent * owners
     away = (
         (row[:, None, None] * owners + me)
@@ -275,7 +286,7 @@
     starts = ((row == 0) & (me == 0))[None, :, None]
     carry = carry + jnp.where(starts, shift.T[:, None, :], 0.0)
     size = columns * extent * rows_here
-    call = pl.pallas_call(
+    return pl.pallas_call(
         quotient_kernel,
         grid=(columns,),
         in_specs=[
@@ -289,8 +300,7 @@
         compiler_params=pltpu.CompilerParams(vmem_limit_bytes=16 << 20),
         cost_estimate=cost(size * 4 * lanes * 6, size * 12),
         name="quotient",
-    )
-    return call(matrix, step, carry, combined), sent
+    )(matrix, step, carry, combined)
 
 
 def transform_tables(extent, rows_here, length):
@@ -317,8 +327,9 @@
     length = extent * rows_here * owners
     first_tables, second_tables = transform_tables(extent, rows_here, length)
     edge = max(1, polys // SHARE)
-    counts = (edge, polys - 2 * edge, edge)
-    starts = (0, edge, polys - edge)
+    head = max(1, edge // 2)
+    counts = (head, polys - head - edge, edge)
+    starts = (0, head, polys - edge)
 
     def opened(i):
         return first_section(coefficients, first_tables, starts[i], counts[i], owners)
@@ -333,10 +344,10 @@
     offsets_here = lax.psum_scatter(
         offsets, ("poly", "limb"), scatter_dimension=1, tiled=True
     )
-    quotient, sent = quotient_section(
-        combined_here, offsets_here, point_index, point_cycle, owners, opened(2)
-    )
-    received.append(passed(sent))
+    quotient = quotient_section(
+        combined_here, offsets_here, point_index, point_cycle, owners
+    )
+    received.append(passed(opened(2)))
     evaluations = second_section(received[0], second_tables, starts[0], polys, None)
     for i in (1, 2):
         evaluations = second_section(

time: 320 us -> 356 us (1.11)
  waiting for transfers between devices: 36.2 us -> 129 us
  blocking collectives: 158 us -> 91.3 us
  other arithmetic: 16 us -> 21.2 us
  starting transfers between devices: 18.2 us -> 23.3 us
    all_gather x1 -> x0, blocking collectives: 66.9 us -> none  [quotient_section(): gathered = lax.all_gather(ends, 'coef')]
    all_to_all x3, waiting for transfers between devices: 36.2 us -> 95.4 us  [passed(): return lax.all_to_all(sent, 'coef', split_axis=0, concat_axis=0, tiled=True)]
    ppermute x0 -> x3, waiting for transfers between devices: none -> 33.9 us  [shared(): arrived.append(lax.ppermute(ends, 'coef', order))]
    ppermute x0 -> x3, starting transfers between devices: none -> 4.95 us  [shared(): arrived.append(lax.ppermute(ends, 'coef', order))]
  transfers between devices with their start and end apart: 6 -> 9, of which waited for: 1 -> 4; matrix products, arithmetic and copies ran while one was open for 4% -> 5% of each run, Pallas kernels for 22% -> 21%
where the time goes in v4:
time: 356 us; the launch traced here: 354 us
  waiting for transfers between devices  129 us (36%)
  blocking collectives  91.3 us (26%)
  Pallas kernels  84.8 us (24%)
  starting transfers between devices  23.3 us (7%)
  other arithmetic  21.2 us (6%)
    all_to_all x3, waiting for transfers between devices, passed(): return lax.all_to_all(sent, 'coef', split_axis=0, concat_axis=0, tiled=True)  95.4 us
    unnamed x1, blocking collectives  91.3 us
    pallas_call x3, Pallas kernels, second_section(): pl.pallas_call(second_kernel, grid=(count, per_target // here), in_specs=...  43.2 us
    ppermute x3, waiting for transfers between devices, shared(): arrived.append(lax.ppermute(ends, 'coef', order))  33.9 us
    pallas_call x3, Pallas kernels, first_section(): pl.pallas_call(first_kernel, grid=(count,), in_specs=[pl.BlockSpec((2 * e...  21.2 us
    all_to_all x3, starting transfers between devices, passed(): return lax.all_to_all(sent, 'coef', split_axis=0, concat_axis=0, tiled=True)  16.6 us
    pallas_call x1, Pallas kernels, combine(): pl.pallas_call(combine_kernel, grid=(extent // 8,), in_specs=[pl.BlockSpe...  15.1 us
  transfers between devices with their start and end apart: 9, of which 4 were waited for; matrix products, arithmetic and copies ran while one was open for 5% of the time, Pallas kernels for 21%

profile of v4, /device:TPU:0, one launch (start us, length us, event | category | flops | bytes accessed | tf_op | source)
XLA Modules:
  0.0 353.6 jit_solution(8416731496234993850)
XLA Ops:
  0.6 0.3 fusion.19
  0.9 2.9 fusion.8
  3.9 0.7 maximum_multiply_fusion.1.mat_ref
  4.5 3.4 first_section.5
  7.9 0.0 copy-done.2
  7.9 6.3 %all-to-all-start.2 = ((f32[4,1,2,8,32,128]{5,4,3,2,1,0:T(8,128)}), f32[4,1,2,8,32,128]{5,4,3,2,1,0:T(8,128)S(1)}, u32[]{:S(2)}, u32[]{:S(2)}) async-start(f32[4,1,2,8,32,128]{5,4,3,2,1,0:T(8,128)} %first_section.5), calls=%async_computation.2 | async-start | bytes 2097152 | tf_op jit(solution)/shard_map/all_to_all | solution.py:338
  14.3 13.3 %first_section.4 = f32[4,9,2,8,32,128]{5,4,3,2,1,0:T(8,128)} custom-call(f32[256,128]{1,0:T(8,128)} %maximum_multiply_fusion.1.mat_ref, f32[128,1024]{1,0:T(8,128)} %get-tuple-element.22.cos_ref, f32[128,1024]{1,0:T(8,128)} %get-tuple-element.21.sin_ref, f32[12,128,1024]{2,1,0:T(8,128)} %x_ref.7), custom_call_target="tpu_custom_call" | custom-call | flops 3623878656 | bytes 14155776 | tf_op jit(solution)/shard_map/first_section/pallas_call | solution.py:54
  27.6 12.4 %all-to-all-done.2.in_ref = f32[4,1,2,8,32,128]{5,4,3,2,1,0:T(8,128)S(1)} async-done(((f32[4,1,2,8,32,128]{5,4,3,2,1,0:T(8,128)}), f32[4,1,2,8,32,128]{5,4,3,2,1,0:T(8,128)S(1)}, u32[]{:S(2)}, u32[]{:S(2)}) %all-to-all-start.2) | async-done | bytes 1048608 | tf_op jit(solution)/shard_map/all_to_all | solution.py:338
  40.0 5.8 %all-to-all-start.1 = ((f32[4,9,2,8,32,128]{5,4,3,2,1,0:T(8,128)}), f32[4,9,2,8,32,128]{5,4,3,2,1,0:T(8,128)}, u32[]{:S(2)}, u32[]{:S(2)}) async-start(f32[4,9,2,8,32,128]{5,4,3,2,1,0:T(8,128)} %first_section.4), calls=%async_computation.1 | async-start | bytes 18874368 | tf_op jit(solution)/shard_map/all_to_all | solution.py:338
  45.8 0.0 copy-done.4
  45.8 0.6 fusion.27.weight_ref
  46.5 15.1 %combine.1 = (f32[4,128,1024]{2,1,0:T(8,128)}, f32[4,128,1024]{2,1,0:T(8,128)}, f32[4,128,1024]{2,1,0:T(8,128)}, f32[4,128,1024]{2,1,0:T(8,128)}) custom-call(f32[16,12]{1,0:T(8,128)} %fusion.27.weight_ref, f32[12,128,1024]{2,1,0:T(8,128)} %x_ref.7), custom_call_target="tpu_custom_call" | custom-call | flops 503316480 | bytes 14680064 | tf_op jit(solution)/shard_map/combine/pallas_call | solution.py:167
  61.6 0.2 collective-permute-start.2
  61.8 1.3 collective-permute-start.1
  63.2 0.2 collective-permute-start
  63.3 0.1 copy.39
  63.4 0.0 copy-done.11
  63.4 0.6 dynamic-slice
  64.6 91.3 %all-reduce = f32[2,16]{1,0:T(2,128)S(1)} all-reduce(f32[2,16]{1,0:T(2,128)S(1)} %multiply_reduce_fusion.2), channel_id=2, replica_groups=mesh['parts'=2,'coef'=4,'poly'=2,'limb'=2] {'poly','limb'}, use_global_device_ids=true, to_apply=%region_3.4.clone | all-reduce | flops 32 | bytes 256
  155.9 0.5 iota_compare_fusion
  156.4 0.5 broadcast_compare_fusion
  156.9 0.5 and_select_fusion
  157.4 0.6 iota_multiply_fusion
  158.0 0.1 dynamic-slice_multiply_fusion
  158.1 0.1 fusion.35
  158.2 0.0 copy-done.6
  158.2 0.5 fusion.32
  158.8 0.1 cosine_multiply_fusion.2
  158.9 0.1 fusion.28
  159.0 4.5 %first_section.3 = f32[4,2,2,8,32,128]{5,4,3,2,1,0:T(8,128)} custom-call(f32[256,128]{1,0:T(8,128)} %maximum_multiply_fusion.1.mat_ref, f32[128,1024]{1,0:T(8,128)} %get-tuple-element.22.cos_ref, f32[128,1024]{1,0:T(8,128)} %get-tuple-element.21.sin_ref, f32[12,128,1024]{2,1,0:T(8,128)} %x_ref.7), custom_call_target="tpu_custom_call" | custom-call | flops 805306368 | bytes 3145728 | tf_op jit(solution)/shard_map/first_section/pallas_call | solution.py:54
  163.5 0.3 fusion.18
  163.8 0.9 maximum_multiply_fusion.mat_ref
  164.7 1.1 negate_select_fusion.5
  165.8 0.8 pad_maximum_fusion.matrix_ref
  166.7 0.1 broadcast_and_fusion.1
  166.7 0.1 broadcast_add_fusion
  166.8 0.2 sine_multiply_fusion.1
  167.0 0.9 fusion.7
  167.9 83.0 %all-to-all-done.1.in_ref = f32[4,9,2,8,32,128]{5,4,3,2,1,0:T(8,128)} async-done(((f32[4,9,2,8,32,128]{5,4,3,2,1,0:T(8,128)}), f32[4,9,2,8,32,128]{5,4,3,2,1,0:T(8,128)}, u32[]{:S(2)}, u32[]{:S(2)}) %all-to-all-start.1) | async-done | bytes 9437216 | tf_op jit(solution)/shard_map/all_to_all | solution.py:338
  250.9 4.5 %all-to-all-start = ((f32[4,2,2,8,32,128]{5,4,3,2,1,0:T(8,128)}), f32[4,2,2,8,32,128]{5,4,3,2,1,0:T(8,128)}, u32[]{:S(2)}, u32[]{:S(2)}) async-start(f32[4,2,2,8,32,128]{5,4,3,2,1,0:T(8,128)} %first_section.3), calls=%async_computation | async-start | bytes 4194304 | tf_op jit(solution)/shard_map/all_to_all | solution.py:338
  255.4 0.1 copy.40
  255.5 0.2 convert_negate_fusion
  255.7 0.0 collective-permute-done.2
  255.7 0.0 copy-start.1
  255.8 0.0 collective-permute-done.1
  255.8 0.0 collective-permute-done
  255.8 1.3 copy-done.1
  257.1 4.1 %multiply_reduce_fusion.1 = (f32[4,128]{1,0:T(4,128)S(1)}, f32[4,128]{1,0:T(4,128)S(1)}, f32[4,128,1024]{2,1,0:T(8,128)S(1)}) fusion(f32[4,1024]{1,0:T(4,128)S(1)} %get-tuple-element.20, f32[4,1024]{1,0:T(4,128)S(1)} %get-tuple-element.19, f32[4,128,1024]{2,1,0:T(8,128)} %copy-done.1, f32[4,128,1024]{2,1,0:T(8,128)} %collective-permute-done.1, ...), kind=kLoop, calls=%fused_computation.1 | loop fusion | flops 3668992 | bytes 10522624 | tf_op jit(solution)/shard_map/reduce_sum | solution.py:253
  261.2 3.8 %collective-permute-start.5 = (f32[2,4,128]{2,1,0:T(4,128)S(1)}, f32[2,4,128]{2,1,0:T(4,128)S(1)}, u32[]{:S(2)}, u32[]{:S(2)}) collective-permute-start(f32[2,4,128]{2,1,0:T(4,128)S(1)} %pad_maximum_fusion.2), channel_id=1, source_target_pairs={{0,12},{4,0},{8,4},{12,8},{1,13},{5,1},{9,5},{13,9},{2,14},{6,2},{... | collective-permute-start | bytes 12296 | tf_op jit(solution)/shard_map/ppermute | solution.py:230
  265.0 0.0 collective-permute-start.4
  265.0 1.1 collective-permute-start.3
  266.2 3.4 second_section.3.rest_0_
  269.6 19.5 %collective-permute-done.5 = f32[2,4,128]{2,1,0:T(4,128)S(1)} collective-permute-done((f32[2,4,128]{2,1,0:T(4,128)S(1)}, f32[2,4,128]{2,1,0:T(4,128)S(1)}, u32[]{:S(2)}, u32[]{:S(2)}) %collective-permute-start.5) | collective-permute-done | bytes 4128 | tf_op jit(solution)/shard_map/ppermute | solution.py:230
  289.1 14.4 %collective-permute-done.4 = f32[2,4,128]{2,1,0:T(4,128)S(1)} collective-permute-done((f32[2,4,128]{2,1,0:T(4,128)S(1)}, f32[2,4,128]{2,1,0:T(4,128)S(1)}, u32[]{:S(2)}, u32[]{:S(2)}) %collective-permute-start.4) | collective-permute-done | bytes 4128 | tf_op jit(solution)/shard_map/ppermute | solution.py:230
  303.5 0.0 collective-permute-done.3
  303.5 0.1 maximum_add_fusion
  303.6 4.6 %subtract_reduce_fusion = (f32[4,128]{1,0:T(4,128)S(1)}, f32[4,128]{1,0:T(4,128)S(1)}) fusion(f32[4,4,128]{2,1,0:T(4,128)S(1)} %get-tuple-element.18, f32[4,4,128]{2,1,0:T(4,128)S(1)} %get-tuple-element.17, s32[4]{0:T(128)S(1)} %copy-done.6, s32[128,4,128]{2,0,1:T(8,128)S(1)} %copy-done.3, f32[4]{0:T(128)S(1)} %get-tuple-element.28, ...), kind=kLoop, calls=%fused_computation.4 | loop fusion | flops 3931136 | bytes 544800 | tf_op jit(solution)/shard_map/reduce_sum | solution.py:283
  308.2 0.1 maximum_divide_fusion
  308.2 0.2 copy.41
  308.4 0.1 select_add_fusion.carry_ref
  308.5 5.3 %quotient.1 = f32[2,4,128,1024]{3,2,1,0:T(8,128)} custom-call(f32[4,128,256]{2,1,0:T(8,128)S(1)} %copy-done, f32[4,2,128]{2,1,0:T(2,128)S(1)} %pad_maximum_fusion.1.step_ref, f32[4,128,2]{2,1,0:T(8,128)S(1)} %select_add_fusion.carry_ref, f32[4,128,1024]{2,1,0:T(8,128)S(1)} %get-tuple-element.14.c_ref), custom_call_target="tpu_custom_call" | custom-call | flops 1610612736 | bytes 6291456 | tf_op jit(solution)/shard_map/quotient/pallas_call | solution.py:289
  313.8 31.8 %second_section.4.rest_0_ = f32[2,32,12,32,128]{4,3,2,1,0:T(8,128)} custom-call(f32[256,256]{1,0:T(8,128)S(1)} %maximum_multiply_fusion.mat_ref, f32[32,128]{1,0:T(8,128)S(1)} %get-tuple-element.32.cos_ref, f32[32,128]{1,0:T(8,128)S(1)} %get-tuple-element.31.sin_ref, ...), custom_call_target="tpu_custom_call", output_to_operand_aliasing={{}: (4, {})} | custom-call | flops 7247757312 | bytes 18874368 | tf_op jit(solution)/shard_map/second_section/pallas_call | solution.py:133
  345.6 0.0 all-to-all-done.in_ref
  345.6 8.0 %second_section.5 = f32[2,32,12,32,128]{4,3,2,1,0:T(8,128)} custom-call(f32[256,256]{1,0:T(8,128)S(1)} %maximum_multiply_fusion.mat_ref, f32[32,128]{1,0:T(8,128)S(1)} %get-tuple-element.32.cos_ref, f32[32,128]{1,0:T(8,128)S(1)} %get-tuple-element.31.sin_ref, f32[4,2,2,8,32,128]{5,4,3,2,1,0:T(8,128)} %all-to-all-done.in_ref, ...), custom_call_target="tpu_custom_call", output_to_operand_aliasing={{}: (4, {})} | custom-call | flops 1610612736 | bytes 4194304 | tf_op jit(solution)/shard_map/second_section/pallas_call | solution.py:133
  (39 shorter events, 0.2 us)
Async XLA Ops:
  0.9 7.0 %copy-start.2 = (f32[128,128]{1,0:T(8,128)}, f32[128,128]{1,0:T(8,128)S(1)}, u32[]{:S(2)}) copy-start(f32[128,128]{1,0:T(8,128)S(1)} %get-tuple-element.30) | copy-start | bytes 196612
  7.9 32.1 %all-to-all-start.2 = ((f32[4,1,2,8,32,128]{5,4,3,2,1,0:T(8,128)}), f32[4,1,2,8,32,128]{5,4,3,2,1,0:T(8,128)S(1)}, u32[]{:S(2)}, u32[]{:S(2)}) async-start(f32[4,1,2,8,32,128]{5,4,3,2,1,0:T(8,128)} %first_section.5), calls=%async_computation.2 | async-start | bytes 2097152 | tf_op jit(solution)/shard_map/all_to_all | solution.py:338
  27.6 18.2 %copy-start.4 = (f32[16,12]{1,0:T(8,128)S(1)}, f32[16,12]{1,0:T(8,128)}, u32[]{:S(2)}) copy-start(f32[16,12]{1,0:T(8,128)} %param.6) | copy-start | bytes 2308
  40.0 210.9 %all-to-all-start.1 = ((f32[4,9,2,8,32,128]{5,4,3,2,1,0:T(8,128)}), f32[4,9,2,8,32,128]{5,4,3,2,1,0:T(8,128)}, u32[]{:S(2)}, u32[]{:S(2)}) async-start(f32[4,9,2,8,32,128]{5,4,3,2,1,0:T(8,128)} %first_section.4), calls=%async_computation.1 | async-start | bytes 18874368 | tf_op jit(solution)/shard_map/all_to_all | solution.py:338
  46.5 17.0 %copy-start.11 = (u32[32]{0:T(128)S(1)}, u32[32]{0:T(128)}, u32[]{:S(2)}) copy-start(u32[32]{0:T(128)} %constant.149) | copy-start | bytes 388
  46.5 18.1 %copy-start.5 = (f32[2,16,12]{1,0,2:T(2,128)S(1)}, f32[2,16,12]{1,0,2:T(2,128)}, u32[]{:S(2)}) copy-start(f32[2,16,12]{1,0,2:T(2,128)} %param.7) | copy-start | bytes 4612
  46.5 111.7 %copy-start.6 = (s32[4]{0:T(128)S(1)}, s32[4]{0:T(128)}, u32[]{:S(2)}) copy-start(s32[4]{0:T(128)} %param.8) | copy-start | bytes 52
  46.5 111.7 %copy-start.10 = (s32[4]{0:T(128)S(1)}, s32[4]{0:T(128)}, u32[]{:S(2)}) copy-start(s32[4]{0:T(128)} %param.9) | copy-start | bytes 52
  61.6 194.1 %collective-permute-start.2 = (f32[4,128,1024]{2,1,0:T(8,128)}, f32[4,128,1024]{2,1,0:T(8,128)S(1)}, u32[]{:S(2)}, u32[]{:S(2)}) collective-permute-start(f32[4,128,1024]{2,1,0:T(8,128)} %get-tuple-element.9), channel_id=1, source_target_pairs={{0,3},{1,0},{2,1},{3,2},{4,7},{5,4},{6,5},{7,6},{8,11},{9,8},{10,9... | collective-permute-start | bytes 6291464 | tf_op jit(solution)/shard_map/ppermute | solution.py:194
  61.8 193.9 %collective-permute-start.1 = (f32[4,128,1024]{2,1,0:T(8,128)}, f32[4,128,1024]{2,1,0:T(8,128)}, u32[]{:S(2)}, u32[]{:S(2)}) collective-permute-start(f32[4,128,1024]{2,1,0:T(8,128)} %get-tuple-element.8), channel_id=1, source_target_pairs={{0,2},{1,3},{2,0},{3,1},{4,6},{5,7},{6,4},{7,5},{8,10},{9,11},{10,... | collective-permute-start | bytes 6291464 | tf_op jit(solution)/shard_map/ppermute | solution.py:194
  63.2 192.6 %collective-permute-start = (f32[4,128,1024]{2,1,0:T(8,128)}, f32[4,128,1024]{2,1,0:T(8,128)}, u32[]{:S(2)}, u32[]{:S(2)}) collective-permute-start(f32[4,128,1024]{2,1,0:T(8,128)} %get-tuple-element.7), channel_id=1, source_target_pairs={{0,1},{1,2},{2,3},{3,0},{4,5},{5,6},{6,7},{7,4},{8,9},{9,10},{10,1... | collective-permute-start | bytes 6291464 | tf_op jit(solution)/shard_map/ppermute | solution.py:194
  163.5 3.1 copy-start.12
  163.5 3.1 copy-start.13
  163.5 3.2 copy-start.8
  163.5 3.2 copy-start.9
  250.9 94.7 %all-to-all-start = ((f32[4,2,2,8,32,128]{5,4,3,2,1,0:T(8,128)}), f32[4,2,2,8,32,128]{5,4,3,2,1,0:T(8,128)}, u32[]{:S(2)}, u32[]{:S(2)}) async-start(f32[4,2,2,8,32,128]{5,4,3,2,1,0:T(8,128)} %first_section.3), calls=%async_computation | async-start | bytes 4194304 | tf_op jit(solution)/shard_map/all_to_all | solution.py:338
  255.7 1.3 copy-start.1
  261.2 27.9 %collective-permute-start.5 = (f32[2,4,128]{2,1,0:T(4,128)S(1)}, f32[2,4,128]{2,1,0:T(4,128)S(1)}, u32[]{:S(2)}, u32[]{:S(2)}) collective-permute-start(f32[2,4,128]{2,1,0:T(4,128)S(1)} %pad_maximum_fusion.2), channel_id=1, source_target_pairs={{0,12},{4,0},{8,4},{12,8},{1,13},{5,1},{9,5},{13,9},{2,14},{6,2},{... | collective-permute-start | bytes 12296 | tf_op jit(solution)/shard_map/ppermute | solution.py:230
  265.0 38.4 %collective-permute-start.4 = (f32[2,4,128]{2,1,0:T(4,128)S(1)}, f32[2,4,128]{2,1,0:T(4,128)S(1)}, u32[]{:S(2)}, u32[]{:S(2)}) collective-permute-start(f32[2,4,128]{2,1,0:T(4,128)S(1)} %pad_maximum_fusion.2), channel_id=1, source_target_pairs={{0,8},{4,12},{8,0},{12,4},{1,9},{5,13},{9,1},{13,5},{2,10},{6,14},... | collective-permute-start | bytes 12296 | tf_op jit(solution)/shard_map/ppermute | solution.py:230
  265.0 38.4 %collective-permute-start.3 = (f32[2,4,128]{2,1,0:T(4,128)S(1)}, f32[2,4,128]{2,1,0:T(4,128)S(1)}, u32[]{:S(2)}, u32[]{:S(2)}) collective-permute-start(f32[2,4,128]{2,1,0:T(4,128)S(1)} %pad_maximum_fusion.2), channel_id=1, source_target_pairs={{0,4},{4,8},{8,12},{12,0},{1,5},{5,9},{9,13},{13,1},{2,6},{6,10},{... | collective-permute-start | bytes 12296 | tf_op jit(solution)/shard_map/ppermute | solution.py:230
  266.2 37.4 %copy-start.3 = (s32[128,4,128]{2,0,1:T(8,128)S(1)}, s32[128,4,128]{2,0,1:T(8,128)}, u32[]{:S(2)}) copy-start(s32[128,4,128]{2,0,1:T(8,128)} %fusion.7) | copy-start | bytes 786436
  266.2 42.0 %copy-start.7 = (f32[4]{0:T(128)S(1)}, f32[4]{0:T(128)}, u32[]{:S(2)}) copy-start(f32[4]{0:T(128)} %get-tuple-element.27) | copy-start | bytes 52
  269.6 39.0 %copy-start = (f32[4,128,256]{2,1,0:T(8,128)S(1)}, f32[4,128,256]{2,1,0:T(8,128)}, u32[]{:S(2)}) copy-start(f32[4,128,256]{2,1,0:T(8,128)} %pad_maximum_fusion.matrix_ref) | copy-start | bytes 1572868

commit v5 on v4

--- a/solution.py
+++ b/solution.py
@@ -26,8 +26,9 @@
     return pl.CostEstimate(flops=flops, bytes_accessed=moved, transcendentals=0)
 
 
-def first_kernel(mat_ref, cos_ref, sin_ref, x_ref, out_ref):
-    targets, _, _, groups, per_target, lanes = out_ref.shape
+def first_kernel(mat_ref, cos_ref, sin_ref, x_ref, *out_refs):
+    targets = len(out_refs)
+    _, _, groups, per_target, lanes = out_refs[0].shape
     extent = targets * per_target
     for g in range(groups):
         cols = slice(g * lanes, (g + 1) * lanes)
@@ -39,8 +40,8 @@
         turned_imag = imag * cos_turn - real * sin_turn
         for t in range(targets):
             rows = slice(t * per_target, (t + 1) * per_target)
-            out_ref[t, 0, 0, g] = turned_real[rows]
-            out_ref[t, 0, 1, g] = turned_imag[rows]
+            out_refs[t][0, 0, g] = turned_real[rows]
+            out_refs[t][0, 1, g] = turned_imag[rows]
 
 
 def first_section(values, tables, start, count, targets):
@@ -48,8 +49,8 @@
     _, extent, rows_here = values.shape
     groups = rows_here // SPLIT_LO
     per_target = extent // targets
-    shape = (targets, count, 2, groups, per_target, SPLIT_LO)
-    block = (targets, 1, 2, groups, per_target, SPLIT_LO)
+    shape = (count, 2, groups, per_target, SPLIT_LO)
+    block = (1, 2, groups, per_target, SPLIT_LO)
     size = count * 2 * extent * rows_here
     return pl.pallas_call(
         first_kernel,
@@ -60,8 +61,8 @@
             pl.BlockSpec((extent, rows_here), lambda p: (0, 0)),
             pl.BlockSpec((1, extent, rows_here), lambda p: (start + p, 0, 0)),
         ],
-        out_specs=pl.BlockSpec(block, lambda p: (0, p, 0, 0, 0, 0)),
-        out_shape=jax.ShapeDtypeStruct(shape, jnp.float32),
+        out_specs=[pl.BlockSpec(block, lambda p: (p, 0, 0, 0, 0))] * targets,
+        out_shape=[jax.ShapeDtypeStruct(shape, jnp.float32)] * targets,
         compiler_params=pltpu.CompilerParams(vmem_limit_bytes=60 << 20),
         cost_estimate=cost(size * extent * 12, size * 6),
         name="first_section",
@@ -95,12 +96,11 @@
     return low + high
 
 
-def second_kernel(mat_ref, cos_ref, sin_ref, in_ref, *rest):
+def second_kernel(sources, mat_ref, cos_ref, sin_ref, *rest):
     out_ref, real_ref, imag_ref = rest[-3:]
-    sources, _, _, groups, here, lanes = in_ref.shape
-    pieces = [
-        (in_ref[s, 0, 0, g], in_ref[s, 0, 1, g]) for s in range(sources) for g in range(groups)
-    ]
+    _, _, groups, here, lanes = rest[0].shape
+    in_refs = [rest[-s % sources] for s in range(sources)]
+    pieces = [(ref[0, 0, g], ref[0, 1, g]) for ref in in_refs for g in range(groups)]
     for v, (real, imag) in enumerate(fft(pieces)):
         cos_turn, sin_turn = cos_ref[v : v + 1], sin_ref[v : v + 1]
         at = pl.ds(v, here, stride=SPLIT_HI)
@@ -114,24 +114,24 @@
 
 def second_section(received, tables, start, total, held):
     matrix, cos_turn, sin_turn = tables
-    sources, count, _, groups, per_target, lanes = received.shape
+    sources = len(received)
+    count, _, groups, per_target, lanes = received[0].shape
     here = min(8, per_target)
     out_shape = jax.ShapeDtypeStruct((2, per_target, total, SPLIT_HI, lanes), jnp.float32)
-    size = received.size
-    operands = [matrix, cos_turn, sin_turn, received]
+    size = sources * received[0].size
+    operands = [matrix, cos_turn, sin_turn, *received]
     in_specs = [
         pl.BlockSpec(matrix.shape, lambda p, k: (0, 0)),
         pl.BlockSpec(cos_turn.shape, lambda p, k: (0, 0)),
         pl.BlockSpec(sin_turn.shape, lambda p, k: (0, 0)),
-        pl.BlockSpec((sources, 1, 2, groups, here, lanes), lambda p, k: (0, p, 0, 0, k, 0)),
-    ]
+    ] + [pl.BlockSpec((1, 2, groups, here, lanes), lambda p, k: (p, 0, 0, k, 0))] * sources
     aliases = {}
     if held is not None:
         operands.append(held)
         in_specs.append(pl.BlockSpec(memory_space=pl.ANY))
-        aliases = {4: 0}
+        aliases = {3 + sources: 0}
     return pl.pallas_call(
-        second_kernel,
+        functools.partial(second_kernel, sources),
         grid=(count, per_target // here),
         in_specs=in_specs,
         out_specs=pl.BlockSpec(
@@ -303,15 +303,17 @@
     )(matrix, step, carry, combined)
 
 
-def transform_tables(extent, rows_here, length):
+def transform_tables(extent, rows_here, length, owners):
     index = jnp.arange(extent, dtype=jnp.int32)
-    cos_table, sin_table = phase_table(index, index, extent)
+    me = lax.axis_index("coef")
+    turned = (index + me * (extent // owners)) % extent
+    cos_table, sin_table = phase_table(turned, index, extent)
     first_matrix = jnp.concatenate([cos_table, -sin_table]) * (1.0 / math.sqrt(extent))
-    row_index = lax.axis_index("coef") * rows_here + jnp.arange(rows_here, dtype=jnp.int32)
-    cos_turn, sin_turn = phase_table(index, row_index, length)
+    row_index = me * rows_here + jnp.arange(rows_here, dtype=jnp.int32)
+    cos_turn, sin_turn = phase_table(turned, row_index, length)
     slow = jnp.arange(SPLIT_HI, dtype=jnp.int32)
     fast = jnp.arange(SPLIT_LO, dtype=jnp.int32)
-    cos_row, sin_row = phase_table(slow, fast, SPLIT_HI * SPLIT_LO)
+    cos_row, sin_row = phase_table(slow, fast + me * rows_here, SPLIT_HI * SPLIT_LO)
     cos_fast, sin_fast = phase_table(fast, fast, SPLIT_LO)
     second_matrix = jnp.concatenate(
         [
@@ -325,7 +327,9 @@
 def shards(owners, coefficients, batch_weights, claimed, point_index, point_cycle):
     polys, extent, rows_here = coefficients.shape
     length = extent * rows_here * owners
-    first_tables, second_tables = transform_tables(extent, rows_here, length)
+    first_tables, second_tables = transform_tables(
+        extent, rows_here, length, owners
+    )
     edge = max(1, polys // SHARE)
     head = max(1, edge // 2)
     counts = (head, polys - head - edge, edge)
@@ -335,7 +339,11 @@
         return first_section(coefficients, first_tables, starts[i], counts[i], owners)
 
     def passed(sent):
-        return lax.all_to_all(sent, "coef", split_axis=0, concat_axis=0, tiled=True)
+        arrived = [sent[0]]
+        for step in range(1, owners):
+            order = [(i, (i + step) % owners) for i in range(owners)]
+            arrived.append(lax.ppermute(sent[step], "coef", order))
+        return arrived
 
     received = [passed(opened(0))]
     combined_here = column_sums(batch_weights, coefficients)

time: 356 us -> 322 us (0.904)
  waiting for transfers between devices: 129 us -> 86.7 us
  starting transfers between devices: 23.3 us -> 30.8 us
    all_to_all x3 -> x0, waiting for transfers between devices: 95.4 us -> none  [passed(): return lax.all_to_all(sent, 'coef', split_axis=0, concat_axis=0, tiled=True)]
    ppermute x0 -> x9, waiting for transfers between devices: none -> 86.7 us  [passed(): arrived.append(lax.ppermute(sent[step], 'coef', order))]
    ppermute x3, waiting for transfers between devices: 33.9 us -> 0.01 us  [shared(): arrived.append(lax.ppermute(ends, 'coef', order))]
    ppermute x0 -> x9, starting transfers between devices: none -> 21.3 us  [passed(): arrived.append(lax.ppermute(sent[step], 'coef', order))]
    all_to_all x3 -> x0, starting transfers between devices: 16.6 us -> none  [passed(): return lax.all_to_all(sent, 'coef', split_axis=0, concat_axis=0, tiled=True)]
  transfers between devices with their start and end apart: 9 -> 15, of which waited for: 4 -> 2; matrix products, arithmetic and copies ran while one was open for 5% -> 5% of each run, Pallas kernels for 21% -> 20%
where the time goes in v5:
time: 322 us; the launch traced here: 318 us
  blocking collectives  92.3 us (29%)
  waiting for transfers between devices  86.7 us (27%)
  Pallas kernels  84.8 us (26%)
  starting transfers between devices  30.8 us (10%)
  other arithmetic  18.7 us (6%)
  local copies, waits for them, and re-layouts  3.34 us (1%)
    unnamed x1, blocking collectives  92.3 us
    ppermute x9, waiting for transfers between devices, passed(): arrived.append(lax.ppermute(sent[step], 'coef', order))  86.7 us
    pallas_call x3, Pallas kernels, second_section(): pl.pallas_call(functools.partial(second_kernel, sources), grid=(count, pe...  43.4 us
    ppermute x9, starting transfers between devices, passed(): arrived.append(lax.ppermute(sent[step], 'coef', order))  21.3 us
    pallas_call x3, Pallas kernels, first_section(): pl.pallas_call(first_kernel, grid=(count,), in_specs=[pl.BlockSpec((2 * e...  21.1 us
    pallas_call x1, Pallas kernels, combine(): pl.pallas_call(combine_kernel, grid=(extent // 8,), in_specs=[pl.BlockSpe...  15.1 us
    ppermute x3, starting transfers between devices, shared(): arrived.append(lax.ppermute(ends, 'coef', order))  7.73 us
  transfers between devices with their start and end apart: 15, of which 2 were waited for; matrix products, arithmetic and copies ran while one was open for 5% of the time, Pallas kernels for 20%

profile of v5, /device:TPU:0, one launch (start us, length us, event | category | flops | bytes accessed | tf_op | source)
XLA Modules:
  0.0 318.1 jit_solution(17062509107710675964)
XLA Ops:
  0.7 0.3 fusion.23
  1.0 3.3 %fusion.5 = (f32[128,1024]{1,0:T(8,128)}, f32[128,1024]{1,0:T(8,128)}) fusion(s32[1024]{0:T(1024)S(1)} %iota_add_fusion, s32[128]{0:T(128)S(1)} %and_select_fusion.1), kind=kLoop, calls=%fused_computation.30 | loop fusion | flops 1835008 | bytes 1053184 | tf_op jit(solution)/shard_map/sin | solution.py:22
  4.3 0.7 maximum_multiply_fusion.1.mat_ref
  5.0 13.2 %first_section.4 = (f32[9,2,8,32,128]{4,3,2,1,0:T(8,128)}, f32[9,2,8,32,128]{4,3,2,1,0:T(8,128)}, f32[9,2,8,32,128]{4,3,2,1,0:T(8,128)}, f32[9,2,8,32,128]{4,3,2,1,0:T(8,128)}) custom-call(f32[256,128]{1,0:T(8,128)} %maximum_multiply_fusion.1.mat_ref, f32[128,1024]{1,0:T(8,128)} %get-tuple-element.46.cos_ref, f32[128,1024]{1,0:T(8,128)} %get-tuple-element.45.sin_ref, ...), custom_call_target="tpu_custom_call" | custom-call | flops 3623878656 | bytes 14155776 | tf_op jit(solution)/shard_map/first_section/pallas_call | solution.py:55
  18.2 3.0 collective-permute-start.3
  21.3 2.6 collective-permute-start.4
  23.9 0.6 fusion.31.weight_ref
  24.5 15.1 %combine.1 = (f32[4,128,1024]{2,1,0:T(8,128)}, f32[4,128,1024]{2,1,0:T(8,128)}, f32[4,128,1024]{2,1,0:T(8,128)}, f32[4,128,1024]{2,1,0:T(8,128)}) custom-call(f32[16,12]{1,0:T(8,128)} %fusion.31.weight_ref, f32[12,128,1024]{2,1,0:T(8,128)} %x_ref.7), custom_call_target="tpu_custom_call" | custom-call | flops 503316480 | bytes 14680064 | tf_op jit(solution)/shard_map/combine/pallas_call | solution.py:167
  39.6 0.4 collective-permute-start.11
  40.0 1.2 collective-permute-start.10
  41.2 0.2 collective-permute-start.9
  41.3 0.3 fusion.24
  41.6 0.1 copy.39
  41.9 92.3 %all-reduce = f32[2,16]{1,0:T(2,128)S(1)} all-reduce(f32[2,16]{1,0:T(2,128)S(1)} %multiply_reduce_fusion.2), channel_id=2, replica_groups=mesh['parts'=2,'coef'=4,'poly'=2,'limb'=2] {'poly','limb'}, use_global_device_ids=true, to_apply=%region_3.4.clone | all-reduce | flops 32 | bytes 256
  134.2 0.6 dynamic-slice
  135.3 0.1 dynamic-slice_multiply_fusion
  135.4 0.1 fusion.40
  135.5 0.1 fusion.37
  135.6 0.1 cosine_multiply_fusion.2
  135.8 3.4 %first_section.5 = (f32[1,2,8,32,128]{4,3,2,1,0:T(8,128)}, f32[1,2,8,32,128]{4,3,2,1,0:T(8,128)}, f32[1,2,8,32,128]{4,3,2,1,0:T(8,128)}, f32[1,2,8,32,128]{4,3,2,1,0:T(8,128)}) custom-call(f32[256,128]{1,0:T(8,128)} %maximum_multiply_fusion.1.mat_ref, f32[128,1024]{1,0:T(8,128)} %get-tuple-element.46.cos_ref, f32[128,1024]{1,0:T(8,128)} %get-tuple-element.45.sin_ref, ...), custom_call_target="tpu_custom_call" | custom-call | flops 402653184 | bytes 1572864 | tf_op jit(solution)/shard_map/first_section/pallas_call | solution.py:55
  139.2 0.3 fusion.21
  139.5 1.1 negate_select_fusion.4
  140.6 0.1 broadcast_and_fusion.1
  140.7 0.1 broadcast_add_fusion
  140.8 0.1 fusion.32
  140.8 0.2 sine_multiply_fusion.1
  141.1 0.9 fusion.4
  141.9 0.9 convert_negate_fusion
  142.9 0.0 collective-permute-done.11
  142.9 1.4 collective-permute-start.5
  144.2 0.0 collective-permute-done.10
  144.2 0.7 collective-permute-start.6
  145.0 0.0 collective-permute-done.9
  145.0 0.3 collective-permute-start.7
  145.3 3.5 %multiply_reduce_fusion.1 = (f32[4,128]{1,0:T(4,128)S(1)}, f32[4,128]{1,0:T(4,128)S(1)}, f32[4,128,1024]{2,1,0:T(8,128)S(1)}) fusion(f32[4,1024]{1,0:T(4,128)S(1)} %get-tuple-element.44, f32[4,1024]{1,0:T(4,128)S(1)} %get-tuple-element.43, f32[4,128,1024]{2,1,0:T(8,128)} %copy-done.6, f32[4,128,1024]{2,1,0:T(8,128)} %collective-permute-done.10, ...), kind=kLoop, calls=%fused_computation.1 | loop fusion | flops 3668992 | bytes 10522624 | tf_op jit(solution)/shard_map/reduce_sum | solution.py:253
  148.8 53.8 %collective-permute-done.6.rest_1_ = f32[1,2,8,32,128]{4,3,2,1,0:T(8,128)S(1)} collective-permute-done((f32[1,2,8,32,128]{4,3,2,1,0:T(8,128)S(1)}, f32[1,2,8,32,128]{4,3,2,1,0:T(8,128)S(1)}, u32[]{:S(2)}, u32[]{:S(2)}) %collective-permute-start.6) | collective-permute-done | bytes 262176 | tf_op jit(solution)/shard_map/ppermute | solution.py:345
  202.7 7.9 %collective-permute-start.8 = (f32[1,2,8,32,128]{4,3,2,1,0:T(8,128)}, f32[1,2,8,32,128]{4,3,2,1,0:T(8,128)}, u32[]{:S(2)}, u32[]{:S(2)}) collective-permute-start(f32[1,2,8,32,128]{4,3,2,1,0:T(8,128)} %get-tuple-element.29), channel_id=1, source_target_pairs={{0,12},{4,0},{8,4},{12,8},{1,13},{5,1},{9,5},{13,9},{2,14},{6,2},{... | collective-permute-start | bytes 786440 | tf_op jit(solution)/shard_map/ppermute | solution.py:345
  210.6 32.8 %collective-permute-done.7.rest_2_ = f32[1,2,8,32,128]{4,3,2,1,0:T(8,128)S(1)} collective-permute-done((f32[1,2,8,32,128]{4,3,2,1,0:T(8,128)S(1)}, f32[1,2,8,32,128]{4,3,2,1,0:T(8,128)S(1)}, u32[]{:S(2)}, u32[]{:S(2)}) %collective-permute-start.7) | collective-permute-done | bytes 262176 | tf_op jit(solution)/shard_map/ppermute | solution.py:345
  243.4 0.7 copy-done.3
  244.1 7.2 %collective-permute-start.14 = (f32[2,4,128]{2,1,0:T(4,128)S(1)}, f32[2,4,128]{2,1,0:T(4,128)S(1)}, u32[]{:S(2)}, u32[]{:S(2)}) collective-permute-start(f32[2,4,128]{2,1,0:T(4,128)S(1)} %pad_maximum_fusion.2), channel_id=1, source_target_pairs={{0,12},{4,0},{8,4},{12,8},{1,13},{5,1},{9,5},{13,9},{2,14},{6,2},{... | collective-permute-start | bytes 12296 | tf_op jit(solution)/shard_map/ppermute | solution.py:230
  251.3 4.4 %first_section.3 = (f32[2,2,8,32,128]{4,3,2,1,0:T(8,128)}, f32[2,2,8,32,128]{4,3,2,1,0:T(8,128)}, f32[2,2,8,32,128]{4,3,2,1,0:T(8,128)}, f32[2,2,8,32,128]{4,3,2,1,0:T(8,128)}) custom-call(f32[256,128]{1,0:T(8,128)} %maximum_multiply_fusion.1.mat_ref, f32[128,1024]{1,0:T(8,128)} %get-tuple-element.46.cos_ref, f32[128,1024]{1,0:T(8,128)} %get-tuple-element.45.sin_ref, ...), custom_call_target="tpu_custom_call" | custom-call | flops 805306368 | bytes 3145728 | tf_op jit(solution)/shard_map/first_section/pallas_call | solution.py:55
  255.7 0.1 copy.40
  255.8 0.0 collective-permute-done.8.rest_3_
  255.8 0.0 collective-permute-start.13
  255.8 0.0 collective-permute-done.14
  255.8 0.6 collective-permute-start.12
  256.4 0.9 copy-done.4
  257.4 4.6 %second_section.3.rest_4_ = f32[2,32,12,32,128]{4,3,2,1,0:T(8,128)} custom-call(f32[256,256]{1,0:T(8,128)S(1)} %maximum_multiply_fusion.mat_ref, f32[32,128]{1,0:T(8,128)S(1)} %get-tuple-element.56.cos_ref, f32[32,128]{1,0:T(8,128)S(1)} %get-tuple-element.55.sin_ref, f32[1,2,8,32,128]{4,3,2,1,0:T(8,128)S(1)} %copy-done.2, ...), custom_call_target="tpu_custom_call" | custom-call | flops 805306368 | bytes 2097152 | tf_op jit(solution)/shard_map/second_section/pallas_call | solution.py:133
  261.9 0.0 collective-permute-done.13
  261.9 2.9 collective-permute-start
  264.8 0.0 collective-permute-done.12
  264.8 1.0 collective-permute-start.1
  265.8 0.1 maximum_add_fusion
  265.9 4.6 %subtract_reduce_fusion = (f32[4,128]{1,0:T(4,128)S(1)}, f32[4,128]{1,0:T(4,128)S(1)}) fusion(f32[4,4,128]{2,1,0:T(4,128)S(1)} %get-tuple-element.42, f32[4,4,128]{2,1,0:T(4,128)S(1)} %get-tuple-element.41, s32[4]{0:T(128)S(1)} %copy-done.11, s32[128,4,128]{2,0,1:T(8,128)S(1)} %copy-done.7, f32[4]{0:T(128)S(1)} %get-tuple-element.52, ...), kind=kLoop, calls=%fused_computation.4 | loop fusion | flops 3931136 | bytes 544800 | tf_op jit(solution)/shard_map/reduce_sum | solution.py:283
  270.5 0.1 maximum_divide_fusion
  270.6 0.9 copy.41
  271.4 1.0 select_add_fusion.carry_ref
  272.5 5.3 %quotient.1 = f32[2,4,128,1024]{3,2,1,0:T(8,128)} custom-call(f32[4,128,256]{2,1,0:T(8,128)S(1)} %pad_maximum_fusion.matrix_ref, f32[4,2,128]{2,1,0:T(2,128)S(1)} %pad_maximum_fusion.1.step_ref, f32[4,128,2]{2,1,0:T(8,128)S(1)} %select_add_fusion.carry_ref, f32[4,128,1024]{2,1,0:T(8,128)S(1)} %get-tuple-element.38.c_ref), custom_call_target="tpu_custom_call" | custom-call | flops 1610612736 | bytes 6291456 | tf_op jit(solution)/shard_map/quotient/pallas_call | solution.py:289
  277.8 1.5 collective-permute-start.2
  279.2 0.0 collective-permute-done.4.rest_2_
  279.3 0.0 collective-permute-done.5.rest_3_
  279.3 31.2 %second_section.4.rest_4_ = f32[2,32,12,32,128]{4,3,2,1,0:T(8,128)} custom-call(f32[256,256]{1,0:T(8,128)S(1)} %maximum_multiply_fusion.mat_ref, f32[32,128]{1,0:T(8,128)S(1)} %get-tuple-element.56.cos_ref, f32[32,128]{1,0:T(8,128)S(1)} %get-tuple-element.55.sin_ref, f32[9,2,8,32,128]{4,3,2,1,0:T(8,128)S(1)} %copy-done, ...), custom_call_target="tpu_custom_call", output_to_operand_aliasing={{}: (7, {})} | custom-call | flops 7247757312 | bytes 18874368 | tf_op jit(solution)/shard_map/second_section/pallas_call | solution.py:133
  310.5 0.0 collective-permute-done.2.rest_3_
  310.5 7.6 %second_section.5 = f32[2,32,12,32,128]{4,3,2,1,0:T(8,128)} custom-call(f32[256,256]{1,0:T(8,128)S(1)} %maximum_multiply_fusion.mat_ref, f32[32,128]{1,0:T(8,128)S(1)} %get-tuple-element.56.cos_ref, f32[32,128]{1,0:T(8,128)S(1)} %get-tuple-element.55.sin_ref, f32[2,2,8,32,128]{4,3,2,1,0:T(8,128)S(1)} %copy-done.1, ...), custom_call_target="tpu_custom_call", output_to_operand_aliasing={{}: (7, {})} | custom-call | flops 1610612736 | bytes 4194304 | tf_op jit(solution)/shard_map/second_section/pallas_call | solution.py:133
  (60 shorter events, 0.3 us)
Async XLA Ops:
  5.0 18.9 %copy-start.9 = (f32[16,12]{1,0:T(8,128)S(1)}, f32[16,12]{1,0:T(8,128)}, u32[]{:S(2)}) copy-start(f32[16,12]{1,0:T(8,128)} %param.6) | copy-start | bytes 2308
  18.2 259.5 %collective-permute-start.3 = (f32[9,2,8,32,128]{4,3,2,1,0:T(8,128)}, f32[9,2,8,32,128]{4,3,2,1,0:T(8,128)}, u32[]{:S(2)}, u32[]{:S(2)}) collective-permute-start(f32[9,2,8,32,128]{4,3,2,1,0:T(8,128)} %get-tuple-element.23), channel_id=1, source_target_pairs={{0,4},{4,8},{8,12},{12,0},{1,5},{5,9},{9,13},{13,1},{2,6},{6,10},{... | collective-permute-start | bytes 7077896 | tf_op jit(solution)/shard_map/ppermute | solution.py:345
  21.3 258.0 %collective-permute-start.4 = (f32[9,2,8,32,128]{4,3,2,1,0:T(8,128)}, f32[9,2,8,32,128]{4,3,2,1,0:T(8,128)}, u32[]{:S(2)}, u32[]{:S(2)}) collective-permute-start(f32[9,2,8,32,128]{4,3,2,1,0:T(8,128)} %get-tuple-element.24), channel_id=1, source_target_pairs={{0,8},{4,12},{8,0},{12,4},{1,9},{5,13},{9,1},{13,5},{2,10},{6,14},... | collective-permute-start | bytes 7077896 | tf_op jit(solution)/shard_map/ppermute | solution.py:345
  24.5 17.4 %copy-start.10 = (f32[2,16,12]{1,0,2:T(2,128)S(1)}, f32[2,16,12]{1,0,2:T(2,128)}, u32[]{:S(2)}) copy-start(f32[2,16,12]{1,0,2:T(2,128)} %param.7) | copy-start | bytes 4612
  24.5 109.7 %copy-start.16 = (u32[32]{0:T(128)S(1)}, u32[32]{0:T(128)}, u32[]{:S(2)}) copy-start(u32[32]{0:T(128)} %constant.159) | copy-start | bytes 388
  24.5 111.0 %copy-start.11 = (s32[4]{0:T(128)S(1)}, s32[4]{0:T(128)}, u32[]{:S(2)}) copy-start(s32[4]{0:T(128)} %param.8) | copy-start | bytes 52
  24.5 111.0 %copy-start.12 = (s32[4]{0:T(128)S(1)}, s32[4]{0:T(128)}, u32[]{:S(2)}) copy-start(s32[4]{0:T(128)} %param.9) | copy-start | bytes 52
  39.6 103.2 %collective-permute-start.11 = (f32[4,128,1024]{2,1,0:T(8,128)}, f32[4,128,1024]{2,1,0:T(8,128)S(1)}, u32[]{:S(2)}, u32[]{:S(2)}) collective-permute-start(f32[4,128,1024]{2,1,0:T(8,128)} %get-tuple-element.33), channel_id=1, source_target_pairs={{0,3},{1,0},{2,1},{3,2},{4,7},{5,4},{6,5},{7,6},{8,11},{9,8},{10,9... | collective-permute-start | bytes 6291464 | tf_op jit(solution)/shard_map/ppermute | solution.py:194
  40.0 104.2 %collective-permute-start.10 = (f32[4,128,1024]{2,1,0:T(8,128)}, f32[4,128,1024]{2,1,0:T(8,128)}, u32[]{:S(2)}, u32[]{:S(2)}) collective-permute-start(f32[4,128,1024]{2,1,0:T(8,128)} %get-tuple-element.32), channel_id=1, source_target_pairs={{0,2},{1,3},{2,0},{3,1},{4,6},{5,7},{6,4},{7,5},{8,10},{9,11},{10,... | collective-permute-start | bytes 6291464 | tf_op jit(solution)/shard_map/ppermute | solution.py:194
  41.2 103.8 %collective-permute-start.9 = (f32[4,128,1024]{2,1,0:T(8,128)}, f32[4,128,1024]{2,1,0:T(8,128)}, u32[]{:S(2)}, u32[]{:S(2)}) collective-permute-start(f32[4,128,1024]{2,1,0:T(8,128)} %get-tuple-element.31), channel_id=1, source_target_pairs={{0,1},{1,2},{2,3},{3,0},{4,5},{5,6},{6,7},{7,4},{8,9},{9,10},{10,1... | collective-permute-start | bytes 6291464 | tf_op jit(solution)/shard_map/ppermute | solution.py:194
  139.1 5.1 %copy-start.15 = (f32[1,2,8,32,128]{4,3,2,1,0:T(8,128)S(1)}, f32[1,2,8,32,128]{4,3,2,1,0:T(8,128)}, u32[]{:S(2)}) copy-start(f32[1,2,8,32,128]{4,3,2,1,0:T(8,128)} %get-tuple-element.27) | copy-start | bytes 786436
  139.2 5.8 %copy-start.14 = (f32[1,2,8,32,128]{4,3,2,1,0:T(8,128)S(1)}, f32[1,2,8,32,128]{4,3,2,1,0:T(8,128)}, u32[]{:S(2)}) copy-start(f32[1,2,8,32,128]{4,3,2,1,0:T(8,128)} %get-tuple-element.28) | copy-start | bytes 786436
  139.2 6.2 %copy-start.5 = (f32[4,128,1024]{2,1,0:T(8,128)S(1)}, f32[4,128,1024]{2,1,0:T(8,128)}, u32[]{:S(2)}) copy-start(f32[4,128,1024]{2,1,0:T(8,128)} %get-tuple-element.30) | copy-start | bytes 6291460
  142.9 2.4 copy-start.6
  142.9 136.4 %collective-permute-start.5 = (f32[9,2,8,32,128]{4,3,2,1,0:T(8,128)}, f32[9,2,8,32,128]{4,3,2,1,0:T(8,128)}, u32[]{:S(2)}, u32[]{:S(2)}) collective-permute-start(f32[9,2,8,32,128]{4,3,2,1,0:T(8,128)} %get-tuple-element.25), channel_id=1, source_target_pairs={{0,12},{4,0},{8,4},{12,8},{1,13},{5,1},{9,5},{13,9},{2,14},{6,2},{... | collective-permute-start | bytes 7077896 | tf_op jit(solution)/shard_map/ppermute | solution.py:345
  144.2 58.4 %collective-permute-start.6 = (f32[1,2,8,32,128]{4,3,2,1,0:T(8,128)S(1)}, f32[1,2,8,32,128]{4,3,2,1,0:T(8,128)S(1)}, u32[]{:S(2)}, u32[]{:S(2)}) collective-permute-start(f32[1,2,8,32,128]{4,3,2,1,0:T(8,128)S(1)} %copy-done.15), channel_id=1, source_target_pairs={{0,4},{4,8},{8,12},{12,0},{1,5},{5,9},{9,13},{13,1},{2,6},{6,10},{... | collective-permute-start | bytes 786440 | tf_op jit(solution)/shard_map/ppermute | solution.py:345
  145.0 98.4 %collective-permute-start.7 = (f32[1,2,8,32,128]{4,3,2,1,0:T(8,128)S(1)}, f32[1,2,8,32,128]{4,3,2,1,0:T(8,128)S(1)}, u32[]{:S(2)}, u32[]{:S(2)}) collective-permute-start(f32[1,2,8,32,128]{4,3,2,1,0:T(8,128)S(1)} %copy-done.14), channel_id=1, source_target_pairs={{0,8},{4,12},{8,0},{12,4},{1,9},{5,13},{9,1},{13,5},{2,10},{6,14},... | collective-permute-start | bytes 786440 | tf_op jit(solution)/shard_map/ppermute | solution.py:345
  202.7 53.1 %collective-permute-start.8 = (f32[1,2,8,32,128]{4,3,2,1,0:T(8,128)}, f32[1,2,8,32,128]{4,3,2,1,0:T(8,128)}, u32[]{:S(2)}, u32[]{:S(2)}) collective-permute-start(f32[1,2,8,32,128]{4,3,2,1,0:T(8,128)} %get-tuple-element.29), channel_id=1, source_target_pairs={{0,12},{4,0},{8,4},{12,8},{1,13},{5,1},{9,5},{13,9},{2,14},{6,2},{... | collective-permute-start | bytes 786440 | tf_op jit(solution)/shard_map/ppermute | solution.py:345
  210.6 45.8 %copy-start.2 = (f32[1,2,8,32,128]{4,3,2,1,0:T(8,128)S(1)}, f32[1,2,8,32,128]{4,3,2,1,0:T(8,128)}, u32[]{:S(2)}) copy-start(f32[1,2,8,32,128]{4,3,2,1,0:T(8,128)} %get-tuple-element.26.rest_0_) | copy-start | bytes 786436
  243.4 0.7 copy-start.3
  244.1 11.7 %collective-permute-start.14 = (f32[2,4,128]{2,1,0:T(4,128)S(1)}, f32[2,4,128]{2,1,0:T(4,128)S(1)}, u32[]{:S(2)}, u32[]{:S(2)}) collective-permute-start(f32[2,4,128]{2,1,0:T(4,128)S(1)} %pad_maximum_fusion.2), channel_id=1, source_target_pairs={{0,12},{4,0},{8,4},{12,8},{1,13},{5,1},{9,5},{13,9},{2,14},{6,2},{... | collective-permute-start | bytes 12296 | tf_op jit(solution)/shard_map/ppermute | solution.py:230
  255.8 6.1 %collective-permute-start.13 = (f32[2,4,128]{2,1,0:T(4,128)S(1)}, f32[2,4,128]{2,1,0:T(4,128)S(1)}, u32[]{:S(2)}, u32[]{:S(2)}) collective-permute-start(f32[2,4,128]{2,1,0:T(4,128)S(1)} %pad_maximum_fusion.2), channel_id=1, source_target_pairs={{0,8},{4,12},{8,0},{12,4},{1,9},{5,13},{9,1},{13,5},{2,10},{6,14},... | collective-permute-start | bytes 12296 | tf_op jit(solution)/shard_map/ppermute | solution.py:230
  255.8 9.0 %collective-permute-start.12 = (f32[2,4,128]{2,1,0:T(4,128)S(1)}, f32[2,4,128]{2,1,0:T(4,128)S(1)}, u32[]{:S(2)}, u32[]{:S(2)}) collective-permute-start(f32[2,4,128]{2,1,0:T(4,128)S(1)} %pad_maximum_fusion.2), channel_id=1, source_target_pairs={{0,4},{4,8},{8,12},{12,0},{1,5},{5,9},{9,13},{13,1},{2,6},{6,10},{... | collective-permute-start | bytes 12296 | tf_op jit(solution)/shard_map/ppermute | solution.py:230
  256.4 1.0 copy-start.4
  257.4 8.5 %copy-start.7 = (s32[128,4,128]{2,0,1:T(8,128)S(1)}, s32[128,4,128]{2,0,1:T(8,128)}, u32[]{:S(2)}) copy-start(s32[128,4,128]{2,0,1:T(8,128)} %fusion.4) | copy-start | bytes 786436
  257.4 8.5 %copy-start.8 = (f32[128,4,128]{2,0,1:T(8,128)S(1)}, f32[128,4,128]{2,0,1:T(8,128)}, u32[]{:S(2)}) copy-start(f32[128,4,128]{2,0,1:T(8,128)} %convert_negate_fusion) | copy-start | bytes 786436
  261.9 48.5 %collective-permute-start = (f32[2,2,8,32,128]{4,3,2,1,0:T(8,128)}, f32[2,2,8,32,128]{4,3,2,1,0:T(8,128)S(1)}, u32[]{:S(2)}, u32[]{:S(2)}) collective-permute-start(f32[2,2,8,32,128]{4,3,2,1,0:T(8,128)} %get-tuple-element.19), channel_id=1, source_target_pairs={{0,4},{4,8},{8,12},{12,0},{1,5},{5,9},{9,13},{13,1},{2,6},{6,10},{... | collective-permute-start | bytes 1572872 | tf_op jit(solution)/shard_map/ppermute | solution.py:345
  264.8 45.6 %collective-permute-start.1 = (f32[2,2,8,32,128]{4,3,2,1,0:T(8,128)}, f32[2,2,8,32,128]{4,3,2,1,0:T(8,128)}, u32[]{:S(2)}, u32[]{:S(2)}) collective-permute-start(f32[2,2,8,32,128]{4,3,2,1,0:T(8,128)} %get-tuple-element.20), channel_id=1, source_target_pairs={{0,8},{4,12},{8,0},{12,4},{1,9},{5,13},{9,1},{13,5},{2,10},{6,14},... | collective-permute-start | bytes 1572872 | tf_op jit(solution)/shard_map/ppermute | solution.py:345
  272.5 5.3 %copy-start.13 = (f32[2,2,8,32,128]{4,3,2,1,0:T(8,128)S(1)}, f32[2,2,8,32,128]{4,3,2,1,0:T(8,128)}, u32[]{:S(2)}) copy-start(f32[2,2,8,32,128]{4,3,2,1,0:T(8,128)} %get-tuple-element.21) | copy-start | bytes 1572868
  272.5 6.8 %copy-start = (f32[9,2,8,32,128]{4,3,2,1,0:T(8,128)S(1)}, f32[9,2,8,32,128]{4,3,2,1,0:T(8,128)}, u32[]{:S(2)}) copy-start(f32[9,2,8,32,128]{4,3,2,1,0:T(8,128)} %get-tuple-element.22.rest_0_) | copy-start | bytes 7077892
  277.8 32.7 %collective-permute-start.2 = (f32[2,2,8,32,128]{4,3,2,1,0:T(8,128)S(1)}, f32[2,2,8,32,128]{4,3,2,1,0:T(8,128)S(1)}, u32[]{:S(2)}, u32[]{:S(2)}) collective-permute-start(f32[2,2,8,32,128]{4,3,2,1,0:T(8,128)S(1)} %copy-done.13), channel_id=1, source_target_pairs={{0,12},{4,0},{8,4},{12,8},{1,13},{5,1},{9,5},{13,9},{2,14},{6,2},{... | collective-permute-start | bytes 1572872 | tf_op jit(solution)/shard_map/ppermute | solution.py:345
  279.3 31.2 %copy-start.1 = (f32[2,2,8,32,128]{4,3,2,1,0:T(8,128)S(1)}, f32[2,2,8,32,128]{4,3,2,1,0:T(8,128)}, u32[]{:S(2)}) copy-start(f32[2,2,8,32,128]{4,3,2,1,0:T(8,128)} %get-tuple-element.18.rest_0_) | copy-start | bytes 1572868
